TPU v7x, 32 devices: a whole 2x2x4 slice. The times are simulated.
32 devices in a mesh: groups: 2 (over y), date: 8 (over z, x), strip: 2 (over core).
Axes of the slice: x: 2, y: 2, z: 4, core: 2. Of those that a mesh axis runs over, the one named last changes fastest.
Arguments:
- slc_tiles: float32 [2, 16, 32, 1024], P(None, ('groups', 'date'), None, 'strip'), parts along dimension 1, may hold values from -6 to 6
- coreg_shift: int32 [16, 2], P(('groups', 'date')), parts along dimension 0, may hold values from -16 to 16, as said below
- center_freq: float32 [16], P('groups'), parts along dimension 0, may hold values from -0.2 to 0.2
- filter_taps: float32 [17], replicated, may hold values from 0.05 to 0.4
- owner_table: int32 [16], P('groups'), parts along dimension 0, may hold values from 0 to 7, each once
Outputs:
- phases: float32 [2, 16, 8192], P(None, 'groups', ('date', 'strip')), parts along dimension 1
There are 2 independent parts, one for each index of `groups`. A program takes and returns all parts, laid end to end along the dimension named above; an argument that names none is the same for every part. Nothing has to cross between parts.
Inputs may be any that keep to these rules, and one draw needn't show every extreme that they name: `coreg_shift`: both 16 and -16 occur in every draw. `owner_table`: a permutation: every index of date owns exactly one block.
All inputs are finite; a program needn't handle non-finite values.
Results may differ from a plain program's by a relative error of at most 0.0003.
Values sent between devices are 32-bit elements; how exact they have to be, the bound alone decides.
No kernel may reach another device: no remote copies, remote signals or barrier semaphores. Data moves between devices by JAX's collectives and lax.ppermute only.
A program may use at most 64 MiB of HBM per device.

v0:
```python
import math

import jax
import jax.numpy as jnp
from jax import lax
from jax.sharding import PartitionSpec as P

SMAX = 16
TAPS = 17
ROUNDS = 3
MINI = 8
ITERS = 3


def swapped(value, axis, bit):
    mask = 2**bit
    pairs = [(source, source ^ mask) for source in range(lax.axis_size(axis))]
    return lax.ppermute(value, axis, pairs)


def padded_2(value, sides, width):
    for axis, dim in sides:
        peers, length = (lax.axis_size(axis), value.shape[dim])
        up = [(i, (i + 1) % peers) for i in range(peers - 1)]
        down = [(j, i) for i, j in up]
        last = lax.slice_in_dim(value, length - width, length, axis=dim)
        leading = lax.slice_in_dim(value, 0, width, axis=dim)
        before = lax.ppermute(last, axis, up)
        after = lax.ppermute(leading, axis, down)
        value = jnp.concatenate([before, value, after], axis=dim)
    return value


def look_mean(field):
    layout = field.shape
    folded = field.reshape(layout[:-2] + (layout[-2] // 2, 2, layout[-1] // 2, 2))
    return jnp.sum(folded, axis=(-3, -1)) * 0.25


def partner_view(field, stride):
    layout = field.shape
    folded = field.reshape((layout[0] // (2 * stride), 2, stride) + layout[1:])
    return jnp.flip(folded, axis=1).reshape(layout)


def pair_terms(lower_re, lower_im, stride):
    layout = lower_re.shape
    folded_re = lower_re.reshape((layout[0] // stride, stride) + layout[1:])
    folded_im = lower_im.reshape((layout[0] // stride, stride) + layout[1:])
    full_shape = (2 * layout[0],) + layout[1:]
    terms_re = jnp.stack([folded_re, folded_re], axis=1).reshape(full_shape)
    terms_im = jnp.stack([folded_im, -folded_im], axis=1).reshape(full_shape)
    return (terms_re, terms_im)


def link_phase(intensity, pair_list):
    vec_re = jnp.ones_like(intensity)
    vec_im = jnp.zeros_like(intensity)
    layout = intensity.shape
    for sweep_step in range(ITERS):
        next_re = intensity * vec_re
        next_im = intensity * vec_im
        for terms_re, terms_im, stride in pair_list:
            other_re = partner_view(vec_re, stride)
            other_im = partner_view(vec_im, stride)
            next_re = next_re + terms_re * other_re - terms_im * other_im
            next_im = next_im + terms_re * other_im + terms_im * other_re
        energy = (next_re * next_re + next_im * next_im).reshape(
            (layout[0] // MINI, MINI) + layout[1:]
        )
        length = jnp.sqrt(jnp.sum(energy, axis=1, keepdims=True))
        factor = jnp.broadcast_to(1.0 / jnp.maximum(length, 1.0), energy.shape).reshape(layout)
        vec_re = next_re * factor
        vec_im = next_im * factor
    return (vec_re, vec_im)


def link_block(received):
    date_count = received.shape[1]
    item_count = received.shape[2]
    pair_list = []
    for round_bit in range(ROUNDS):
        stride = 1 << round_bit
        fields = received[2 * round_bit : 2 * round_bit + 2].reshape(
            2, date_count // (2 * stride), 2, stride, item_count
        )
        lower_ifg = jnp.moveaxis(fields, 2, 3).reshape(2, date_count // 2, 2, item_count)
        terms_re, terms_im = pair_terms(lower_ifg[0], lower_ifg[1], stride)
        pair_list.append((terms_re, terms_im, stride))
    brightness = jnp.moveaxis(received[2 * ROUNDS : 2 * ROUNDS + 2], 0, 1)
    vec_re, vec_im = link_phase(brightness, pair_list)
    return jnp.stack([vec_re, vec_im])


def band_matrix(filter_taps, rotation, block_len):
    tap_count = filter_taps.shape[0]
    offsets = jnp.arange(tap_count, dtype=jnp.float32) - tap_count // 2
    tap_re = filter_taps * jnp.cos(rotation * offsets)
    tap_im = filter_taps * jnp.sin(rotation * offsets)
    lag_grid = (
        jnp.arange(block_len + tap_count - 1, dtype=jnp.int32)[:, None]
        - jnp.arange(block_len, dtype=jnp.int32)[None, :]
    )
    picked = lag_grid[:, :, None] == jnp.arange(tap_count, dtype=jnp.int32)[None, None, :]
    mat_re = jnp.sum(jnp.where(picked, tap_re, 0.0), axis=-1)
    mat_im = jnp.sum(jnp.where(picked, tap_im, 0.0), axis=-1)
    upper_half = jnp.concatenate([mat_re, mat_im], axis=1)
    lower_half = jnp.concatenate([-mat_im, mat_re], axis=1)
    return jnp.concatenate([upper_half, lower_half], axis=0)


def band_filter(extended, matrix, block_len, tap_reach):
    components, row_count, total_cols = extended.shape
    out_cols = total_cols - 2 * tap_reach
    nblocks = out_cols // block_len
    left_rim = extended[:, :, :out_cols].reshape(components, row_count, nblocks, block_len)[
        ..., :tap_reach
    ]
    middle = extended[:, :, tap_reach : tap_reach + out_cols].reshape(
        components, row_count, nblocks, block_len
    )
    right_rim = extended[:, :, 2 * tap_reach :].reshape(components, row_count, nblocks, block_len)[
        ..., block_len - tap_reach :
    ]
    windows = jnp.concatenate([left_rim, middle, right_rim], axis=-1)
    joined = jnp.concatenate([windows[0], windows[1]], axis=-1).reshape(row_count * nblocks, -1)
    product = jnp.dot(
        joined, matrix, precision=lax.Precision.HIGHEST, preferred_element_type=jnp.float32
    )
    product = product.reshape(row_count, nblocks, 2, block_len)
    return (
        product[:, :, 0].reshape(row_count, out_cols),
        product[:, :, 1].reshape(row_count, out_cols),
    )


def trade(payload, round_bit):
    return swapped(payload, "date", round_bit)


def shards(slc_tiles, coreg_shift, center_freq, filter_taps, owner_table):
    tap_reach = TAPS // 2
    margin = SMAX + tap_reach
    own_tile = slc_tiles[:, 0]
    row_count = own_tile.shape[1]
    strip_cols = own_tile.shape[2]
    block_len = math.gcd(strip_cols, 128)
    date_count = lax.axis_size("date")
    position = lax.axis_index("date")
    padded = padded_2(own_tile, (("strip", 2),), margin)
    line_blocks = coreg_shift.shape[1]
    grouped = padded.reshape(2, line_blocks, row_count // line_blocks, padded.shape[2])

    def shift_block(segment, amount):
        return lax.dynamic_slice_in_dim(segment, SMAX + amount, strip_cols + 2 * tap_reach, axis=2)

    resampled = jax.vmap(shift_block, in_axes=(1, 0), out_axes=1)(grouped, coreg_shift[0])
    resampled = resampled.reshape(2, row_count, strip_cols + 2 * tap_reach)
    centre = resampled[:, :, tap_reach : tap_reach + strip_cols]
    brightness = look_mean(centre[0] * centre[0] + centre[1] * centre[1])
    half_rows = row_count // 2
    pixel_count = half_rows // 2 * (strip_cols // 2)
    block_pixels = pixel_count // date_count
    bright_fields = brightness.reshape(2, date_count, block_pixels)
    date_ids = jnp.arange(date_count, dtype=jnp.int32)
    own_freq = jnp.sum(jnp.where(date_ids == position, center_freq, 0.0))
    inverse = jnp.zeros((date_count,), jnp.int32).at[owner_table].set(date_ids)
    ifg_fields = []
    for round_bit in range(ROUNDS):
        stride = 1 << round_bit
        parity = position // stride % 2
        partner = jnp.bitwise_xor(position, stride)
        partner_freq = jnp.sum(jnp.where(date_ids == partner, center_freq, 0.0))
        rotation = jnp.pi * (partner_freq - own_freq)
        whole_re, whole_im = band_filter(
            resampled, band_matrix(filter_taps, rotation, block_len), block_len, tap_reach
        )
        filtered = jnp.stack([whole_re, whole_im])
        outgoing = lax.dynamic_slice_in_dim(filtered, (1 - parity) * half_rows, half_rows, axis=1)
        kept_half = lax.dynamic_slice_in_dim(filtered, parity * half_rows, half_rows, axis=1)
        arrived = trade(outgoing, round_bit)
        mine_re, mine_im = (kept_half[0], kept_half[1])
        theirs_re, theirs_im = (arrived[0], arrived[1])
        is_lower = parity == 0
        first_re = jnp.where(is_lower, mine_re, theirs_re)
        first_im = jnp.where(is_lower, mine_im, theirs_im)
        second_re = jnp.where(is_lower, theirs_re, mine_re)
        second_im = jnp.where(is_lower, theirs_im, mine_im)
        ifg_re = look_mean(first_re * second_re + first_im * second_im)
        ifg_im = look_mean(first_im * second_re - first_re * second_im)
        round_fields = jnp.stack([ifg_re, ifg_im]).reshape(2, date_count, block_pixels)
        ifg_fields.append(round_fields)
    outgoing_all = jnp.take(jnp.concatenate(ifg_fields + [bright_fields], axis=0), inverse, axis=1)
    linked = link_block(
        lax.all_to_all(outgoing_all, "date", split_axis=1, concat_axis=1, tiled=True)
    )
    return linked.reshape(2, date_count, 2 * block_pixels)


def solution(mesh):
    in_specs = (
        P(None, ("groups", "date"), None, "strip"),
        P(("groups", "date"), None),
        P("groups"),
        P(),
        P("groups"),
    )
    out_specs = P(None, "groups", ("date", "strip"))
    return jax.shard_map(shards, mesh=mesh, in_specs=in_specs, out_specs=out_specs, check_vma=False)
```

profile of v0, /device:TPU:0, one launch (start us, length us, event | category | flops | bytes accessed | tf_op | source)
XLA Modules:
  0.0 62.4 jit_solution(8768502680218335158)
XLA Ops:
  0.0 0.9 %fusion.65 = (f32[2,32,24]{2,1,0:T(8,128)S(1)}, f32[2,32,24]{2,1,0:T(8,128)S(1)}) fusion(f32[2,32,512]{2,1,0:T(8,128)} %bitcast.407), kind=kLoop, calls=%fused_computation.199 | loop fusion | bytes 24576 | tf_op jit(solution)/shard_map/slice | solution.py:26
  0.9 2.4 %collective-permute-start = (f32[2,32,24]{2,1,0:T(8,128)S(1)}, f32[2,32,24]{2,1,0:T(8,128)S(1)}, u32[]{:S(2)}, u32[]{:S(2)}) collective-permute-start(f32[2,32,24]{2,1,0:T(8,128)S(1)} %get-tuple-element.47), channel_id=1, source_target_pairs={{0,1},{2,3},{4,5},{6,7},{8,9},{10,11},{12,13},{14,15},{16,17},{18,... | collective-permute-start | bytes 18440 | tf_op jit(solution)/shard_map/ppermute | solution.py:28
  3.3 1.3 %collective-permute-start.1 = (f32[2,32,24]{2,1,0:T(8,128)S(1)}, f32[2,32,24]{2,1,0:T(8,128)S(1)}, u32[]{:S(2)}, u32[]{:S(2)}) collective-permute-start(f32[2,32,24]{2,1,0:T(8,128)S(1)} %get-tuple-element.48), channel_id=1, source_target_pairs={{1,0},{3,2},{5,4},{7,6},{9,8},{11,10},{13,12},{15,14},{17,16},{19,... | collective-permute-start | bytes 18440 | tf_op jit(solution)/shard_map/ppermute | solution.py:29
  4.6 0.7 %compare_select_fusion.2 = s32[8]{0:T(128)S(1)} fusion(s32[8]{0:T(128)} %param.9), kind=kLoop, calls=%fused_computation.163 | loop fusion | flops 24 | bytes 64 | tf_op jit(solution)/shard_map/select_n | solution.py:167
  5.3 0.6 scatter_custom_fusion
  5.9 1.3 %fusion.45 = (f32[]{:T(128)}, f32[]{:T(128)}, f32[]{:T(128)}, f32[]{:T(128)}) fusion(f32[8]{0:T(128)} %param.7, s32[]{:T(128)S(6)} %xor.11, s32[]{:T(128)S(6)} %axis_index.15, s32[]{:T(128)S(6)} %xor.9, s32[]{:T(128)S(6)} %xor.10), kind=kLoop, calls=%fused_computation.175 | loop fusion | flops 92 | bytes 64 | tf_op jit(solution)/shard_map/reduce_sum | solution.py:173
  11.2 0.7 %or_bitcast_fusion = s32[2]{0:T(128)S(1)} fusion(s32[1,2]{1,0:T(1,128)} %param.6), kind=kLoop, calls=%fused_computation.177 | loop fusion | flops 18 | bytes 16 | tf_op jit(solution)/shard_map/vmap()/gather | solution.py:155
  11.9 0.7 %cosine_multiply_fusion.2 = (f32[17]{0:T(128)S(1)}, f32[17]{0:T(128)S(1)}, f32[17]{0:T(128)S(1)}, f32[17]{0:T(128)S(1)}, f32[17]{0:T(128)S(1)}, /*index=5*/f32[17]{0:T(128)S(1)}) fusion(f32[17]{0:T(128)} %param.8, f32[]{:T(128)S(6)} %mul.430, f32[]{:T(128)S(6)} %mul.445, f32[]{:T(128)S(6)} %mul.460), kind=kLoop, calls=%fused_computation.183 | loop fusion | flops 170 | bytes 488 | tf_op jit(solution)/shard_map/mul | solution.py:98
  12.6 1.0 %select_reduce_fusion = (f32[144,128]{1,0:T(8,128)S(1)}, f32[144,128]{1,0:T(8,128)S(1)}, f32[144,128]{1,0:T(8,128)S(1)}, f32[144,128]{1,0:T(8,128)S(1)}, f32[144,128]{1,0:T(8,128)S(1)}, /*index=5*/f32[144,128]{1,0:T(8,128)S(1)}) fusion(f32[17]{0:T(128)S(1)} %get-tuple-element.68, s32[144,128]{1,0:T(8,128)S(1)} %iota_subtract_fusion, ...), kind=kLoop, calls=%fused_computation.3 | loop fusion | flops 3962880 | bytes 516504 | tf_op jit(solution)/shard_map/reduce_sum | solution.py:106
  13.9 0.1 pad_maximum_fusion.1
  14.0 0.8 %copy.94 = f32[2,2,16,560]{2,0,1,3:T(2,128)S(1)} copy(f32[2,2,16,560]{3,2,1,0:T(8,128)S(1)} %pad_maximum_fusion.1) | data formatting | bytes 286720 | tf_op jit(solution)/shard_map/concatenate | solution.py:30
  14.8 2.0 %gather_fusion.1 = f32[2,2,16,528]{2,1,3,0:T(2,128)S(1)} fusion(f32[2,2,16,560]{2,1,0,3:T(2,128)S(1)} %bitcast.403, s32[2]{0:T(128)S(1)} %or_bitcast_fusion), kind=kCustom, calls=%fused_computation.1 | custom fusion | bytes 270368 | tf_op jit(solution)/shard_map/vmap()/gather | solution.py:155
  16.8 0.5 copy.95
  17.3 0.1 fusion.61
  17.5 0.1 fusion.12
  17.6 0.1 slice.195
  17.9 0.2 pad_maximum_fusion
  18.1 0.4 fusion
  18.6 0.1 fusion.7
  18.8 3.5 %collective-permute-start.4 = (f32[2,16,512]{2,0,1:T(2,128)S(1)}, f32[2,16,512]{2,0,1:T(2,128)S(1)}, u32[]{:S(2)}, u32[]{:S(2)}) collective-permute-start(f32[2,16,512]{2,0,1:T(2,128)S(1)} %get-tuple-element.36), channel_id=1, source_target_pairs={{0,8},{2,10},{4,12},{6,14},{8,0},{10,2},{12,4},{14,6},{1,9},{3,11}... | collective-permute-start | bytes 196616 | tf_op jit(solution)/shard_map/ppermute | solution.py:18
  22.2 0.4 fusion.2
  22.8 0.1 fusion.9
  22.9 1.6 %collective-permute-start.3 = (f32[2,16,512]{2,0,1:T(2,128)S(1)}, f32[2,16,512]{2,0,1:T(2,128)S(1)}, u32[]{:S(2)}, u32[]{:S(2)}) collective-permute-start(f32[2,16,512]{2,0,1:T(2,128)S(1)} %get-tuple-element.40), channel_id=1, source_target_pairs={{0,4},{2,6},{4,0},{6,2},{8,12},{10,14},{12,8},{14,10},{1,5},{3,7},... | collective-permute-start | bytes 196616 | tf_op jit(solution)/shard_map/ppermute | solution.py:18
  24.6 0.4 fusion.4
  25.1 0.1 fusion.11
  25.2 1.6 %collective-permute-start.2 = (f32[2,16,512]{2,0,1:T(2,128)S(1)}, f32[2,16,512]{2,0,1:T(2,128)S(1)}, u32[]{:S(2)}, u32[]{:S(2)}) collective-permute-start(f32[2,16,512]{2,0,1:T(2,128)S(1)} %get-tuple-element.44), channel_id=1, source_target_pairs={{0,2},{2,0},{4,6},{6,4},{8,10},{10,8},{12,14},{14,12},{1,3},{3,1},... | collective-permute-start | bytes 196616 | tf_op jit(solution)/shard_map/ppermute | solution.py:18
  26.8 5.5 %add.228 = f32[16,2,256,2]{3,2,1,0:T(8,128)} reshape(f32[1,32,512]{2,1,0:T(8,128)S(1)} %fusion.12) | data formatting | bytes 131072 | tf_op jit(solution)/shard_map/add | solution.py:160
  32.3 2.8 %reduce_sum.196 = f32[16,256]{1,0:T(8,128)S(1)} reduce(f32[16,2,256,2]{3,2,1,0:T(8,128)} %add.228, f32[]{:T(128)} %constant.95.clone.1), dimensions={1,3}, to_apply=%region_17.18 | reduce | flops 12288 | bytes 81924 | tf_op jit(solution)/shard_map/reduce_sum | solution.py:37
  35.1 0.3 subtract_reduce_fusion
  35.4 2.1 %add.226 = f32[8,2,256,2]{3,2,1,0:T(8,128)S(1)} reshape(f32[16,512]{1,0:T(8,128)S(1)} %get-tuple-element.6) | data formatting | bytes 65536 | tf_op jit(solution)/shard_map/add | solution.py:189
  37.5 0.3 reduce_sum.194
  37.8 2.1 %sub.173 = f32[8,2,256,2]{3,2,1,0:T(8,128)S(1)} reshape(f32[16,512]{1,0:T(8,128)S(1)} %get-tuple-element.5) | data formatting | bytes 65536 | tf_op jit(solution)/shard_map/sub | solution.py:190
  39.9 0.3 reduce_sum.195
  40.3 0.3 subtract_reduce_fusion.1
  40.6 2.1 %add.221 = f32[8,2,256,2]{3,2,1,0:T(8,128)S(1)} reshape(f32[16,512]{1,0:T(8,128)S(1)} %get-tuple-element.8) | data formatting | bytes 65536 | tf_op jit(solution)/shard_map/add | solution.py:189
  42.7 0.3 reduce_sum.189
  43.0 2.1 %sub.168 = f32[8,2,256,2]{3,2,1,0:T(8,128)S(1)} reshape(f32[16,512]{1,0:T(8,128)S(1)} %get-tuple-element.7) | data formatting | bytes 65536 | tf_op jit(solution)/shard_map/sub | solution.py:190
  45.1 0.3 reduce_sum.190
  45.6 0.3 subtract_reduce_fusion.2
  45.8 2.1 %add.216 = f32[8,2,256,2]{3,2,1,0:T(8,128)S(1)} reshape(f32[16,512]{1,0:T(8,128)S(1)} %get-tuple-element.10) | data formatting | bytes 65536 | tf_op jit(solution)/shard_map/add | solution.py:189
  47.9 0.3 reduce_sum.184
  48.3 2.1 %sub.163 = f32[8,2,256,2]{3,2,1,0:T(8,128)S(1)} reshape(f32[16,512]{1,0:T(8,128)S(1)} %get-tuple-element.9) | data formatting | bytes 65536 | tf_op jit(solution)/shard_map/sub | solution.py:190
  50.4 0.3 reduce_sum.185
  50.9 0.6 gather_fusion
  51.5 9.3 %all_to_all.5 = f32[8,8,256]{2,0,1:T(8,128)S(1)} all-to-all(f32[8,8,256]{2,0,1:T(8,128)S(1)} %select_bitcast_fusion), channel_id=1, replica_groups=mesh['groups'=2,'date'=8,'strip'=2] {'date'}, dimensions={1} | all-to-all | bytes 131072 | tf_op jit(solution)/shard_map/all_to_all | solution.py:195
  61.4 0.1 add_reduce_fusion.4
  61.6 0.1 add_reduce_fusion.3
  61.8 0.6 pad_maximum_fusion.2
  (91 shorter events, 1.3 us)
Async XLA Ops:
  0.0 13.9 %copy-start = (f32[2,1,32,512]{3,2,1,0:T(8,128)S(1)}, f32[2,1,32,512]{3,2,1,0:T(8,128)}, u32[]{:S(2)}) copy-start(f32[2,1,32,512]{3,2,1,0:T(8,128)} %param.5) | copy-start | bytes 393220
  0.9 13.0 %collective-permute-start = (f32[2,32,24]{2,1,0:T(8,128)S(1)}, f32[2,32,24]{2,1,0:T(8,128)S(1)}, u32[]{:S(2)}, u32[]{:S(2)}) collective-permute-start(f32[2,32,24]{2,1,0:T(8,128)S(1)} %get-tuple-element.47), channel_id=1, source_target_pairs={{0,1},{2,3},{4,5},{6,7},{8,9},{10,11},{12,13},{14,15},{16,17},{18,... | collective-permute-start | bytes 18440 | tf_op jit(solution)/shard_map/ppermute | solution.py:28
  3.3 10.6 %collective-permute-start.1 = (f32[2,32,24]{2,1,0:T(8,128)S(1)}, f32[2,32,24]{2,1,0:T(8,128)S(1)}, u32[]{:S(2)}, u32[]{:S(2)}) collective-permute-start(f32[2,32,24]{2,1,0:T(8,128)S(1)} %get-tuple-element.48), channel_id=1, source_target_pairs={{1,0},{3,2},{5,4},{7,6},{9,8},{11,10},{13,12},{15,14},{17,16},{19,... | collective-permute-start | bytes 18440 | tf_op jit(solution)/shard_map/ppermute | solution.py:29
  18.8 16.4 %collective-permute-start.4 = (f32[2,16,512]{2,0,1:T(2,128)S(1)}, f32[2,16,512]{2,0,1:T(2,128)S(1)}, u32[]{:S(2)}, u32[]{:S(2)}) collective-permute-start(f32[2,16,512]{2,0,1:T(2,128)S(1)} %get-tuple-element.36), channel_id=1, source_target_pairs={{0,8},{2,10},{4,12},{6,14},{8,0},{10,2},{12,4},{14,6},{1,9},{3,11}... | collective-permute-start | bytes 196616 | tf_op jit(solution)/shard_map/ppermute | solution.py:18
  22.9 17.4 %collective-permute-start.3 = (f32[2,16,512]{2,0,1:T(2,128)S(1)}, f32[2,16,512]{2,0,1:T(2,128)S(1)}, u32[]{:S(2)}, u32[]{:S(2)}) collective-permute-start(f32[2,16,512]{2,0,1:T(2,128)S(1)} %get-tuple-element.40), channel_id=1, source_target_pairs={{0,4},{2,6},{4,0},{6,2},{8,12},{10,14},{12,8},{14,10},{1,5},{3,7},... | collective-permute-start | bytes 196616 | tf_op jit(solution)/shard_map/ppermute | solution.py:18
  25.2 20.3 %collective-permute-start.2 = (f32[2,16,512]{2,0,1:T(2,128)S(1)}, f32[2,16,512]{2,0,1:T(2,128)S(1)}, u32[]{:S(2)}, u32[]{:S(2)}) collective-permute-start(f32[2,16,512]{2,0,1:T(2,128)S(1)} %get-tuple-element.44), channel_id=1, source_target_pairs={{0,2},{2,0},{4,6},{6,4},{8,10},{10,8},{12,14},{14,12},{1,3},{3,1},... | collective-permute-start | bytes 196616 | tf_op jit(solution)/shard_map/ppermute | solution.py:18
where the time goes:
time: 62.7 us; the launch traced here: 62.4 us
  local copies, waits for them, and re-layouts  24.4 us (39%)
  other arithmetic  12.2 us (19%)
  starting transfers between devices  10.4 us (17%)
  blocking collectives  9.28 us (15%)
  between operations  4.92 us (8%)
  matrix products  1.25 us (2%)
    all_to_all x1, blocking collectives, shards(): lax.all_to_all(outgoing_all, 'date', split_axis=1, concat_axis=1, tiled=T...  9.28 us
    ppermute x3, starting transfers between devices, swapped(): return lax.ppermute(value, axis, pairs)  6.67 us
    sub x3, local copies, waits for them, and re-layouts, shards(): ifg_im = look_mean(first_im * second_re - first_re * second_im)  6.25 us
    add x3, local copies, waits for them, and re-layouts, shards(): ifg_re = look_mean(first_re * second_re + first_im * second_im)  6.25 us
    add x1, local copies, waits for them, and re-layouts, shards(): brightness = look_mean(centre[0] * centre[0] + centre[1] * centre[1])  5.48 us
    reduce_sum x7, other arithmetic, look_mean(): return jnp.sum(folded, axis=(-3, -1)) * 0.25  4.88 us
    ppermute x1, starting transfers between devices, padded_2(): before = lax.ppermute(last, axis, up)  2.39 us
    gather x1, local copies, waits for them, and re-layouts, shift_block(): lax.dynamic_slice_in_dim(segment, SMAX + amount, strip_cols + 2 * tap_rea...  2.01 us
  transfers between devices with their start and end apart: 5, of which 0 were waited for; matrix products, arithmetic and copies ran while one was open for 40% of the time, Pallas kernels for 0%

commit v1 on v0

v1 whole, which is shorter than its diff:
```python
import functools

import jax
import jax.numpy as jnp
from jax import lax
from jax.experimental import pallas as pl
from jax.experimental.pallas import tpu as pltpu
from jax.sharding import PartitionSpec as P

SMAX = 16
TAPS = 17
ROUNDS = 3
MINI = 8
ITERS = 3
LANES = 128
REACH = TAPS // 2
VMEM_LIMIT = 16 * 1024 * 1024


def smem():
    return pl.BlockSpec(memory_space=pltpu.SMEM)


def vmem():
    return pl.BlockSpec(memory_space=pltpu.VMEM)


def params():
    return pltpu.CompilerParams(vmem_limit_bytes=VMEM_LIMIT)


def coef_kernel(freq_ref, out_ref):
    date = lax.broadcasted_iota(jnp.int32, (MINI, LANES), 0)
    lane = lax.broadcasted_iota(jnp.int32, (MINI, LANES), 1)

    def freq_of(index):
        total = jnp.zeros((MINI, LANES), jnp.float32)
        for d in range(MINI):
            total = jnp.where(index == d, freq_ref[d], total)
        return total

    own = freq_of(date)
    rotation = jnp.zeros((MINI, LANES), jnp.float32)
    for r in range(ROUNDS):
        q = jnp.pi * (freq_of(jnp.bitwise_xor(date, 1 << r)) - own)
        rotation = jnp.where(lane // REACH == r, q, rotation)
    angle = rotation * (lane % REACH + 1).astype(jnp.float32)
    cosine, sine = jnp.cos(angle), jnp.sin(angle)
    for j in range(ROUNDS * REACH):
        out_ref[2 * j] = jnp.broadcast_to(cosine[:, j : j + 1], (MINI, LANES))
        out_ref[2 * j + 1] = jnp.broadcast_to(sine[:, j : j + 1], (MINI, LANES))


def pack_kernel(slot_ref, shift_ref, place_ref, own_ref, other_ref, out_ref):
    _, rows, cols = own_ref.shape
    blocks = shift_ref.shape[1]
    block_rows = rows // blocks
    share = block_rows // MINI
    height = 2 * blocks * share
    first = place_ref[0] == 0
    for e in range(blocks):
        offset = LANES - REACH + shift_ref[0, e]
        for c in range(2):
            lines = pl.ds(e * block_rows, block_rows)
            left = jnp.where(first, 0.0, other_ref[c, lines, cols - LANES : cols])
            right = jnp.where(first, other_ref[c, lines, 0:LANES], 0.0)
            line = jnp.concatenate([left, own_ref[c, lines, :], right], axis=1)
            total = cols + 2 * LANES
            moved = pltpu.roll(line, total - offset, 1)
            for q in range(MINI):
                for b in range(out_ref.shape[1] // height):
                    row = b * height + (c * blocks + e) * share
                    out_ref[slot_ref[q], row : row + share, :] = moved[
                        q * share : (q + 1) * share, b * LANES : (b + 1) * LANES
                    ]


def partner(value, stride):
    if 2 * stride == MINI:
        return pltpu.roll(value, stride, 0)
    date = lax.broadcasted_iota(jnp.int32, value.shape, 0)
    up = pltpu.roll(value, MINI - stride, 0)
    down = pltpu.roll(value, stride, 0)
    return jnp.where((date // stride) % 2 == 0, up, down)


def link_kernel(tap_ref, coef_ref, data_ref, out_ref, look_ref):
    blocks = 2
    nb = 2 * out_ref.shape[2] // blocks // LANES
    height = 4 * blocks
    stride = (nb + 1) * height
    lane = lax.broadcasted_iota(jnp.int32, (MINI, LANES), 1)
    fields = 2 * ROUNDS + 1
    half = 2 * LANES
    for e in range(blocks):
        for b in range(nb):
            sums = [None] * fields
            for p in range(2):
                pieces = []
                for c in range(2):
                    row = (c * blocks + e) * 2 + p
                    pieces.append(
                        [
                            data_ref[pl.ds((b + i) * height + row, MINI, stride=stride), :]
                            for i in range(2)
                        ]
                    )

                def at(c, t):
                    here, there = pieces[c]
                    if t == 0:
                        return here
                    both = jnp.where(lane < t, there, here)
                    return pltpu.roll(both, LANES - t, 1)

                centre = [at(c, REACH) for c in range(2)]
                acc = [[tap_ref[REACH] * centre[c] for c in range(2)] for _ in range(ROUNDS)]
                for k in range(1, REACH + 1):
                    plus = [tap_ref[REACH + k] * at(c, REACH + k) for c in range(2)]
                    minus = [tap_ref[REACH - k] * at(c, REACH - k) for c in range(2)]
                    even = [plus[c] + minus[c] for c in range(2)]
                    odd = [plus[c] - minus[c] for c in range(2)]
                    for r in range(ROUNDS):
                        j = r * REACH + k - 1
                        cosine, sine = coef_ref[2 * j], coef_ref[2 * j + 1]
                        acc[r][0] = acc[r][0] + (cosine * even[0] - sine * odd[1])
                        acc[r][1] = acc[r][1] + (cosine * even[1] + sine * odd[0])
                terms = []
                for r in range(ROUNDS):
                    y_re, y_im = acc[r]
                    z_re, z_im = partner(y_re, 1 << r), partner(y_im, 1 << r)
                    terms.append(y_re * z_re + y_im * z_im)
                    terms.append(y_im * z_re - y_re * z_im)
                terms.append(centre[0] * centre[0] + centre[1] * centre[1])
                sums = [t if s is None else s + t for s, t in zip(sums, terms)]
            for f in range(fields):
                row = ((e * nb + b) // 2 * fields + f) * MINI
                look_ref[row : row + MINI, pl.ds(b % 2 * LANES, LANES)] = sums[f]
    value = look_ref[...]
    source = lax.broadcasted_iota(jnp.int32, (half, LANES), 0)
    target = lax.broadcasted_iota(jnp.int32, (half, LANES), 1)
    weights = jnp.where(source // 2 == target, 0.25, 0.0).astype(jnp.bfloat16)
    looked = jnp.zeros((value.shape[0], LANES), jnp.float32)
    for _ in range(3):
        part = value.astype(jnp.bfloat16)
        value = value - part.astype(jnp.float32)
        looked = looked + jnp.dot(part, weights, preferred_element_type=jnp.float32)
    for g in range(blocks * nb // 2):
        base = g * fields * MINI
        field = [looked[base + f * MINI : base + (f + 1) * MINI] for f in range(fields)]
        vec_re = jnp.ones((MINI, LANES), jnp.float32)
        vec_im = jnp.zeros((MINI, LANES), jnp.float32)
        for _ in range(ITERS):
            next_re = field[-1] * vec_re
            next_im = field[-1] * vec_im
            for r in range(ROUNDS):
                o_re, o_im = partner(vec_re, 1 << r), partner(vec_im, 1 << r)
                t_re, t_im = field[2 * r], field[2 * r + 1]
                next_re = next_re + t_re * o_re - t_im * o_im
                next_im = next_im + t_re * o_im + t_im * o_re
            energy = jnp.sum(next_re * next_re + next_im * next_im, axis=0, keepdims=True)
            factor = 1.0 / jnp.maximum(jnp.sqrt(energy), 1.0)
            vec_re = next_re * factor
            vec_im = next_im * factor
        out_ref[0, :, pl.ds(g * LANES, LANES)] = vec_re
        out_ref[1, :, pl.ds(g * LANES, LANES)] = vec_im


def to_owners(linked, inverse, blocks):
    date_count = lax.axis_size("date")
    position = lax.axis_index("date")
    parts = date_count // MINI
    member = position % MINI
    cut = linked.reshape(2, MINI, blocks, parts, -1)
    own_blocks = lax.dynamic_slice_in_dim(jnp.argsort(inverse), member * parts, parts)
    outgoing = jnp.zeros((date_count, 2, MINI, blocks, cut.shape[-1]), jnp.float32)
    outgoing = outgoing.at[own_blocks].set(jnp.moveaxis(cut, 3, 0))
    arrived = lax.all_to_all(outgoing, "date", split_axis=0, concat_axis=0, tiled=True)
    source = inverse[position] // parts
    arrived = arrived.reshape((parts, MINI) + arrived.shape[1:])
    chosen = lax.dynamic_index_in_dim(arrived, source, axis=1, keepdims=False)
    return jnp.moveaxis(chosen, 1, 0).reshape(2, date_count, -1)


def shards(slc_tiles, coreg_shift, center_freq, filter_taps, owner_table):
    own_tile = slc_tiles[:, 0]
    _, rows, cols = own_tile.shape
    date_count = lax.axis_size("date")
    strips = lax.axis_size("strip")
    blocks = coreg_shift.shape[1]
    share = rows // blocks // MINI
    position = lax.axis_index("date")
    other_tile = lax.ppermute(own_tile, "strip", [(s, strips - 1 - s) for s in range(strips)])
    if date_count == MINI:
        slots, stack, freq = owner_table, None, center_freq
    else:
        slots = jnp.arange(MINI, dtype=jnp.int32)
        stack = [list(range(g, g + MINI)) for g in range(0, date_count, MINI)]
        freq = lax.dynamic_slice_in_dim(center_freq, position // MINI * MINI, MINI)
    coefs = pl.pallas_call(
        coef_kernel,
        out_shape=jax.ShapeDtypeStruct((2 * ROUNDS * REACH, MINI, LANES), jnp.float32),
        in_specs=[smem()],
        out_specs=vmem(),
        compiler_params=params(),
        name="coefs",
    )(freq)
    height = 2 * blocks * share * (cols // LANES + 1)
    packed = pl.pallas_call(
        pack_kernel,
        out_shape=jax.ShapeDtypeStruct((MINI, height, LANES), jnp.float32),
        in_specs=[smem(), smem(), smem(), vmem(), vmem()],
        out_specs=vmem(),
        compiler_params=params(),
        name="pack",
    )(slots, coreg_shift, lax.axis_index("strip")[None], own_tile, other_tile)
    data = lax.all_to_all(
        packed, "date", split_axis=0, concat_axis=0, axis_index_groups=stack, tiled=True
    )
    pixels = blocks * share // 2 * cols // 2
    fields = 2 * ROUNDS + 1
    linked = pl.pallas_call(
        link_kernel,
        out_shape=jax.ShapeDtypeStruct((2, MINI, pixels), jnp.float32),
        in_specs=[smem(), vmem(), vmem()],
        out_specs=vmem(),
        scratch_shapes=[pltpu.VMEM((pixels // LANES * fields * MINI, 2 * LANES), jnp.float32)],
        compiler_params=params(),
        name="link",
    )(filter_taps, coefs, data.reshape(-1, LANES))
    if date_count == MINI:
        return linked
    date_ids = jnp.arange(date_count, dtype=jnp.int32)
    inverse = jnp.zeros((date_count,), jnp.int32).at[owner_table].set(date_ids)
    return to_owners(linked, inverse, blocks)


def solution(mesh):
    in_specs = (
        P(None, ("groups", "date"), None, "strip"),
        P(("groups", "date"), None),
        P("groups"),
        P(),
        P("groups"),
    )
    out_specs = P(None, "groups", ("date", "strip"))
    return jax.shard_map(shards, mesh=mesh, in_specs=in_specs, out_specs=out_specs, check_vma=False)
```

time: 62.7 us -> 21.6 us (0.34)
  local copies, waits for them, and re-layouts: 24.4 us -> 0.92 us
  other arithmetic: 12.2 us -> 0 us
  blocking collectives: 9.28 us -> 0 us
  waiting for transfers between devices: 0.01 us -> 8.22 us
  between operations: 4.92 us -> 0.02 us
  Pallas kernels: 0 us -> 4.4 us
  starting transfers between devices: 10.4 us -> 7.77 us
  matrix products: 1.25 us -> 0 us
    add x4 -> x0, local copies, waits for them, and re-layouts: 11.7 us -> none  [the longest x3 6.25 us: shards(): ifg_re = look_mean(first_re * second_re + first_im * second_im)]
    ppermute x5 -> x1, starting transfers between devices: 10.4 us -> 0.49 us  [shards(): lax.ppermute(own_tile, 'strip', [(s, strips - 1 - s) for s in range(strip...]
    all_to_all x1 -> x0, blocking collectives: 9.28 us -> none  [shards(): lax.all_to_all(outgoing_all, 'date', split_axis=1, concat_axis=1, tiled=T...]
    reduce_sum x12 -> x0, other arithmetic: 7.57 us -> none  [the longest x7 4.88 us: look_mean(): return jnp.sum(folded, axis=(-3, -1)) * 0.25]
    all_to_all x0 -> x1, starting transfers between devices: none -> 7.28 us  [shards(): lax.all_to_all(packed, 'date', split_axis=0, concat_axis=0, axis_index_gr...]
    all_to_all x0 -> x1, waiting for transfers between devices: none -> 7.02 us  [shards(): lax.all_to_all(packed, 'date', split_axis=0, concat_axis=0, axis_index_gr...]
    sub x3 -> x0, local copies, waits for them, and re-layouts: 6.25 us -> none  [shards(): ifg_im = look_mean(first_im * second_re - first_re * second_im)]
    pallas_call x0 -> x3, Pallas kernels: none -> 4.4 us  [the longest x1 2.33 us: shards(): pl.pallas_call(link_kernel, out_shape=jax.ShapeDtypeStruct((2, MINI, pixe...]
  transfers between devices with their start and end apart: 5 -> 2, of which waited for: 0 -> 2; matrix products, arithmetic and copies ran while one was open for 40% -> 0% of each run, Pallas kernels for 0% -> 3%
where the time goes in v1:
time: 21.6 us; the launch traced here: 21.3 us
  waiting for transfers between devices  8.22 us (38%)
  starting transfers between devices  7.77 us (36%)
  Pallas kernels  4.4 us (20%)
  local copies, waits for them, and re-layouts  0.92 us (4%)
    all_to_all x1, starting transfers between devices, shards(): lax.all_to_all(packed, 'date', split_axis=0, concat_axis=0, axis_index_gr...  7.28 us
    all_to_all x1, waiting for transfers between devices, shards(): lax.all_to_all(packed, 'date', split_axis=0, concat_axis=0, axis_index_gr...  7.02 us
    pallas_call x1, Pallas kernels, shards(): pl.pallas_call(link_kernel, out_shape=jax.ShapeDtypeStruct((2, MINI, pixe...  2.33 us
    pallas_call x1, Pallas kernels, shards(): pl.pallas_call(pack_kernel, out_shape=jax.ShapeDtypeStruct((MINI, height,...  1.34 us
    ppermute x1, waiting for transfers between devices, shards(): lax.ppermute(own_tile, 'strip', [(s, strips - 1 - s) for s in range(strip...  1.19 us
    unnamed x10, local copies, waits for them, and re-layouts  0.92 us
    pallas_call x1, Pallas kernels, shards(): pl.pallas_call(coef_kernel, out_shape=jax.ShapeDtypeStruct((2 * ROUNDS *...  0.74 us
    ppermute x1, starting transfers between devices, shards(): lax.ppermute(own_tile, 'strip', [(s, strips - 1 - s) for s in range(strip...  0.49 us
  transfers between devices with their start and end apart: 2, of which 2 were waited for; matrix products, arithmetic and copies ran while one was open for 0% of the time, Pallas kernels for 3%

profile of v1, /device:TPU:0, one launch (start us, length us, event | category | flops | bytes accessed | tf_op | source)
XLA Modules:
  0.0 21.3 jit_solution(3347788190016869219)
XLA Ops:
  0.0 0.5 %collective-permute-start = (f32[2,32,512]{2,1,0:T(8,128)}, f32[2,32,512]{2,1,0:T(8,128)S(1)}, u32[]{:S(2)}, u32[]{:S(2)}) collective-permute-start(f32[2,32,512]{2,1,0:T(8,128)} %bitcast.4), channel_id=1, source_target_pairs={{0,1},{1,0},{2,3},{3,2},{4,5},{5,4},{6,7},{7,6},{8,9},{9,8},{10,11... | collective-permute-start | bytes 393224 | tf_op jit(solution)/shard_map/ppermute | solution.py:193
  0.5 0.0 copy-start.1
  0.5 0.0 copy-start.2
  0.5 1.2 %collective-permute-done.other_ref = f32[2,32,512]{2,1,0:T(8,128)S(1)} collective-permute-done((f32[2,32,512]{2,1,0:T(8,128)}, f32[2,32,512]{2,1,0:T(8,128)S(1)}, u32[]{:S(2)}, u32[]{:S(2)}) %collective-permute-start) | collective-permute-done | bytes 131104 | tf_op jit(solution)/shard_map/ppermute | solution.py:193
  1.7 0.0 copy-done.1
  1.7 0.0 copy-done.2
  1.7 0.0 copy-start
  1.7 0.9 %copy-done = f32[2,1,32,512]{3,2,1,0:T(8,128)S(1)} copy-done((f32[2,1,32,512]{3,2,1,0:T(8,128)S(1)}, f32[2,1,32,512]{3,2,1,0:T(8,128)}, u32[]{:S(2)}) %copy-start) | copy-done | bytes 131096
  2.6 1.3 %pack.1 = f32[8,40,128]{2,1,0:T(8,128)} custom-call(s32[8]{0:T(128)S(1)} %copy-done.1, s32[1,2]{1,0:T(1,128)S(1)} %copy-done.2, s32[1]{0:T(128)} %bitcast.place_ref, f32[2,32,512]{2,1,0:T(8,128)S(1)} %bitcast.5, f32[2,32,512]{2,1,0:T(8,128)S(1)} %collective-permute-done.other_ref), custom_call_target="tpu_custom_call" | custom-call | tf_op jit(solution)/shard_map/pack/pallas_call | solution.py:209
  3.9 0.0 copy-start.3
  3.9 7.3 %all-to-all-start = ((f32[8,40,128]{2,1,0:T(8,128)}), f32[8,40,128]{2,1,0:T(8,128)S(1)}, u32[]{:S(2)}, u32[]{:S(2)}) async-start(f32[8,40,128]{2,1,0:T(8,128)} %pack.1), calls=%async_computation | async-start | bytes 327680 | tf_op jit(solution)/shard_map/all_to_all | solution.py:217
  11.2 0.0 copy-done.3
  11.2 0.7 %coefs.1.coef_ref = f32[48,8,128]{2,1,0:T(8,128)S(1)} custom-call(f32[8]{0:T(128)S(1)} %copy-done.3), custom_call_target="tpu_custom_call" | custom-call | tf_op jit(solution)/shard_map/coefs/pallas_call | solution.py:200
  12.0 0.0 copy-start.4
  12.0 7.0 %all-to-all-done = f32[8,40,128]{2,1,0:T(8,128)S(1)} async-done(((f32[8,40,128]{2,1,0:T(8,128)}), f32[8,40,128]{2,1,0:T(8,128)S(1)}, u32[]{:S(2)}, u32[]{:S(2)}) %all-to-all-start) | async-done | bytes 163872 | tf_op jit(solution)/shard_map/all_to_all | solution.py:217
  19.0 0.0 copy-done.4
  19.0 2.3 %link.1 = f32[2,8,512]{2,1,0:T(8,128)} custom-call(f32[17]{0:T(128)S(1)} %copy-done.4, f32[48,8,128]{2,1,0:T(8,128)S(1)} %coefs.1.coef_ref, f32[320,128]{1,0:T(8,128)S(1)} %bitcast.3), custom_call_target="tpu_custom_call" | custom-call | tf_op jit(solution)/shard_map/link/pallas_call | solution.py:222
Async XLA Ops:
  0.0 1.7 %collective-permute-start = (f32[2,32,512]{2,1,0:T(8,128)}, f32[2,32,512]{2,1,0:T(8,128)S(1)}, u32[]{:S(2)}, u32[]{:S(2)}) collective-permute-start(f32[2,32,512]{2,1,0:T(8,128)} %bitcast.4), channel_id=1, source_target_pairs={{0,1},{1,0},{2,3},{3,2},{4,5},{5,4},{6,7},{7,6},{8,9},{9,8},{10,11... | collective-permute-start | bytes 393224 | tf_op jit(solution)/shard_map/ppermute | solution.py:193
  0.5 1.2 %copy-start.1 = (s32[8]{0:T(128)S(1)}, s32[8]{0:T(128)}, u32[]{:S(2)}) copy-start(s32[8]{0:T(128)} %slot_ref.1) | copy-start | bytes 100
  0.5 1.2 %copy-start.2 = (s32[1,2]{1,0:T(1,128)S(1)}, s32[1,2]{1,0:T(1,128)}, u32[]{:S(2)}) copy-start(s32[1,2]{1,0:T(1,128)} %shift_ref.1) | copy-start | bytes 28
  1.7 0.9 %copy-start = (f32[2,1,32,512]{3,2,1,0:T(8,128)S(1)}, f32[2,1,32,512]{3,2,1,0:T(8,128)}, u32[]{:S(2)}) copy-start(f32[2,1,32,512]{3,2,1,0:T(8,128)} %param.5) | copy-start | bytes 393220
  3.9 7.3 %copy-start.3 = (f32[8]{0:T(128)S(1)}, f32[8]{0:T(128)}, u32[]{:S(2)}) copy-start(f32[8]{0:T(128)} %freq_ref.1) | copy-start | bytes 100
  3.9 15.1 %all-to-all-start = ((f32[8,40,128]{2,1,0:T(8,128)}), f32[8,40,128]{2,1,0:T(8,128)S(1)}, u32[]{:S(2)}, u32[]{:S(2)}) async-start(f32[8,40,128]{2,1,0:T(8,128)} %pack.1), calls=%async_computation | async-start | bytes 327680 | tf_op jit(solution)/shard_map/all_to_all | solution.py:217
  12.0 7.0 %copy-start.4 = (f32[17]{0:T(128)S(1)}, f32[17]{0:T(128)}, u32[]{:S(2)}) copy-start(f32[17]{0:T(128)} %tap_ref.1) | copy-start | bytes 208

commit v2 on v1

v2 whole, which is shorter than its diff:
```python
import jax
import jax.numpy as jnp
from jax import lax
from jax.experimental import pallas as pl
from jax.experimental.pallas import tpu as pltpu
from jax.sharding import PartitionSpec as P

SMAX = 16
TAPS = 17
ROUNDS = 3
MINI = 8
ITERS = 3
LANES = 128
REACH = TAPS // 2
VMEM_LIMIT = 16 * 1024 * 1024


def vmem():
    return pl.BlockSpec(memory_space=pltpu.VMEM)


def hbm():
    return pl.BlockSpec(memory_space=pltpu.HBM)


def in_hbm(value):
    return pltpu.with_memory_space_constraint(value, pltpu.HBM)


def params():
    return pltpu.CompilerParams(vmem_limit_bytes=VMEM_LIMIT)


def prep_kernel(
    freq_hbm, tap_hbm, slot_hbm, shift_hbm, tile_hbm,
    coef_ref, tap_out, slot_out, shift_out, packed_ref,
    freq_ref, tap_ref, slot_ref, shift_ref, tile_ref, sems,
):
    copies = [
        pltpu.make_async_copy(source, target, sems.at[i])
        for i, (source, target) in enumerate(
            (
                (freq_hbm, freq_ref),
                (shift_hbm, shift_ref),
                (slot_hbm, slot_ref),
                (tap_hbm, tap_ref),
                (tile_hbm, tile_ref),
            )
        )
    ]
    for copy in copies:
        copy.start()
    date = lax.broadcasted_iota(jnp.int32, (MINI, LANES), 0)
    lane = lax.broadcasted_iota(jnp.int32, (MINI, LANES), 1)
    for copy in copies[:4]:
        copy.wait()

    def freq_of(index):
        total = jnp.zeros((MINI, LANES), jnp.float32)
        for d in range(MINI):
            total = jnp.where(index == d, freq_ref[d], total)
        return total

    own = freq_of(date)
    rotation = jnp.zeros((MINI, LANES), jnp.float32)
    for r in range(ROUNDS):
        q = jnp.pi * (freq_of(jnp.bitwise_xor(date, 1 << r)) - own)
        rotation = jnp.where(lane // REACH == r, q, rotation)
    angle = rotation * (lane % REACH + 1).astype(jnp.float32)
    cosine, sine = jnp.cos(angle), jnp.sin(angle)
    for j in range(ROUNDS * REACH):
        coef_ref[2 * j] = jnp.broadcast_to(cosine[:, j : j + 1], (MINI, LANES))
        coef_ref[2 * j + 1] = jnp.broadcast_to(sine[:, j : j + 1], (MINI, LANES))
    for t in range(TAPS):
        tap_out[t] = jnp.full((MINI, LANES), tap_ref[t], jnp.float32)
    for q in range(MINI):
        slot_out[q] = jnp.full((MINI, LANES), slot_ref[q], jnp.int32)
    _, rows, cols = tile_ref.shape
    blocks = shift_ref.shape[1]
    block_rows = rows // blocks
    share = block_rows // MINI
    height = 2 * blocks * share
    row = lax.broadcasted_iota(jnp.int32, (MINI, LANES), 0)
    offsets = jnp.zeros((MINI, LANES), jnp.int32)
    for e in range(blocks):
        offsets = jnp.where(row // share % blocks == e, shift_ref[0, e] + SMAX, offsets)
        shift_out[e] = jnp.full((MINI, LANES), shift_ref[0, e] + SMAX, jnp.int32)
    shift_out[blocks] = offsets
    copies[4].wait()
    total = cols + 2 * LANES
    for e in range(blocks):
        offset = LANES - REACH + shift_ref[0, e]
        for c in range(2):
            rim = jnp.zeros((block_rows, LANES), jnp.float32)
            lines = tile_ref[c, e * block_rows : (e + 1) * block_rows, :]
            moved = pltpu.roll(jnp.concatenate([rim, lines, rim], axis=1), total - offset, 1)
            for q in range(MINI):
                for b in range(packed_ref.shape[1] // height):
                    at = b * height + (c * blocks + e) * share
                    packed_ref[slot_ref[q], at : at + share, :] = moved[
                        q * share : (q + 1) * share, b * LANES : (b + 1) * LANES
                    ]


def rim_kernel(place_ref, slot_ref, shift_ref, other_ref, packed_ref, out_ref):
    _, rows, cols = other_ref.shape
    blocks = shift_ref.shape[0] - 1
    block_rows = rows // blocks
    share = block_rows // MINI
    first = place_ref[0] == 0
    lane = lax.broadcasted_iota(jnp.int32, (MINI, LANES), 1)
    reach = SMAX + REACH
    moved = []
    for c in range(2):
        for e in range(blocks):
            lines = pl.ds(e * block_rows, block_rows)
            rim = jnp.where(first, other_ref[c, lines, 0:LANES], other_ref[c, lines, cols - LANES : cols])
            shift = jnp.concatenate([shift_ref[e]] * (block_rows // MINI), axis=0)
            for bit in range((2 * SMAX).bit_length()):
                rim = jnp.where(shift & (1 << bit) != 0, pltpu.roll(rim, LANES - (1 << bit), 1), rim)
            moved.append(pltpu.roll(rim, reach, 1))
    pieces = [
        jnp.concatenate([m[q * share : (q + 1) * share] for m in moved], axis=0) for q in range(MINI)
    ]
    edge = reach - shift_ref[blocks]
    height = 2 * blocks * share
    last = cols // LANES
    side = jnp.where(first, 0, 1)
    masks = {
        0: lane + (1 - side) * 2 * LANES < edge,
        last - 1: lane - side * 4 * LANES >= edge + LANES,
        last: lane - side * 4 * LANES >= edge,
    }
    for j in range(MINI):
        rim = pieces[0]
        for q in range(1, MINI):
            rim = jnp.where(slot_ref[q] == j, pieces[q], rim)
        for b, mask in masks.items():
            at = slice(b * height, (b + 1) * height)
            out_ref[j, at, :] = jnp.where(mask, rim, packed_ref[j, at, :])


def partner(value, stride):
    if 2 * stride == MINI:
        return pltpu.roll(value, stride, 0)
    date = lax.broadcasted_iota(jnp.int32, value.shape, 0)
    up = pltpu.roll(value, MINI - stride, 0)
    down = pltpu.roll(value, stride, 0)
    return jnp.where((date // stride) % 2 == 0, up, down)


def link_kernel(tap_ref, coef_ref, data_ref, out_ref):
    blocks = 2
    nb = 2 * out_ref.shape[2] // blocks // LANES
    height = 4 * blocks
    stride = (nb + 1) * height
    lane = lax.broadcasted_iota(jnp.int32, (MINI, LANES), 1)
    fields = 2 * ROUNDS + 1
    source = lax.broadcasted_iota(jnp.int32, (2 * LANES, LANES), 0)
    target = lax.broadcasted_iota(jnp.int32, (2 * LANES, LANES), 1)
    weights = jnp.where(source // 2 == target, 0.25, 0.0).astype(jnp.bfloat16)

    def sums_of(e, b):
        sums = [None] * fields
        for p in range(2):
            pieces = []
            for c in range(2):
                row = (c * blocks + e) * 2 + p
                pieces.append(
                    [data_ref[pl.ds((b + i) * height + row, MINI, stride=stride), :] for i in range(2)]
                )

            def at(c, t):
                here, there = pieces[c]
                if t == 0:
                    return here
                return pltpu.roll(jnp.where(lane < t, there, here), LANES - t, 1)

            centre = [at(c, REACH) for c in range(2)]
            acc = [[tap_ref[REACH] * centre[c] for c in range(2)] for _ in range(ROUNDS)]
            for k in range(1, REACH + 1):
                plus = [tap_ref[REACH + k] * at(c, REACH + k) for c in range(2)]
                minus = [tap_ref[REACH - k] * at(c, REACH - k) for c in range(2)]
                even = [plus[c] + minus[c] for c in range(2)]
                odd = [plus[c] - minus[c] for c in range(2)]
                for r in range(ROUNDS):
                    j = r * REACH + k - 1
                    cosine, sine = coef_ref[2 * j], coef_ref[2 * j + 1]
                    acc[r][0] = acc[r][0] + (cosine * even[0] - sine * odd[1])
                    acc[r][1] = acc[r][1] + (cosine * even[1] + sine * odd[0])
            terms = []
            for r in range(ROUNDS):
                y_re, y_im = acc[r]
                z_re, z_im = partner(y_re, 1 << r), partner(y_im, 1 << r)
                terms.append(y_re * z_re + y_im * z_im)
                terms.append(y_im * z_re - y_re * z_im)
            terms.append(centre[0] * centre[0] + centre[1] * centre[1])
            sums = [t if s is None else s + t for s, t in zip(sums, terms)]
        return jnp.concatenate(sums, axis=0)

    for g in range(blocks * nb // 2):
        e, b = g // (nb // 2), g % (nb // 2) * 2
        value = jnp.concatenate([sums_of(e, b), sums_of(e, b + 1)], axis=1)
        looked = jnp.zeros((value.shape[0], LANES), jnp.float32)
        for _ in range(3):
            part = value.astype(jnp.bfloat16)
            value = value - part.astype(jnp.float32)
            looked = looked + jnp.dot(part, weights, preferred_element_type=jnp.float32)
        field = [looked[f * MINI : (f + 1) * MINI] for f in range(fields)]
        vec_re = jnp.ones((MINI, LANES), jnp.float32)
        vec_im = jnp.zeros((MINI, LANES), jnp.float32)
        for _ in range(ITERS):
            next_re = field[-1] * vec_re
            next_im = field[-1] * vec_im
            for r in range(ROUNDS):
                o_re, o_im = partner(vec_re, 1 << r), partner(vec_im, 1 << r)
                t_re, t_im = field[2 * r], field[2 * r + 1]
                next_re = next_re + t_re * o_re - t_im * o_im
                next_im = next_im + t_re * o_im + t_im * o_re
            energy = jnp.sum(next_re * next_re + next_im * next_im, axis=0, keepdims=True)
            factor = 1.0 / jnp.maximum(jnp.sqrt(energy), 1.0)
            vec_re = next_re * factor
            vec_im = next_im * factor
        out_ref[0, :, pl.ds(g * LANES, LANES)] = vec_re
        out_ref[1, :, pl.ds(g * LANES, LANES)] = vec_im


def to_owners(linked, inverse, blocks):
    date_count = lax.axis_size("date")
    position = lax.axis_index("date")
    parts = date_count // MINI
    member = position % MINI
    cut = linked.reshape(2, MINI, blocks, parts, -1)
    own_blocks = lax.dynamic_slice_in_dim(jnp.argsort(inverse), member * parts, parts)
    outgoing = jnp.zeros((date_count, 2, MINI, blocks, cut.shape[-1]), jnp.float32)
    outgoing = outgoing.at[own_blocks].set(jnp.moveaxis(cut, 3, 0))
    arrived = lax.all_to_all(outgoing, "date", split_axis=0, concat_axis=0, tiled=True)
    source = inverse[position] // parts
    arrived = arrived.reshape((parts, MINI) + arrived.shape[1:])
    chosen = lax.dynamic_index_in_dim(arrived, source, axis=1, keepdims=False)
    return jnp.moveaxis(chosen, 1, 0).reshape(2, date_count, -1)


def shards(slc_tiles, coreg_shift, center_freq, filter_taps, owner_table):
    own_tile = slc_tiles[:, 0]
    _, rows, cols = own_tile.shape
    date_count = lax.axis_size("date")
    strips = lax.axis_size("strip")
    blocks = coreg_shift.shape[1]
    share = rows // blocks // MINI
    position = lax.axis_index("date")
    other_tile = lax.ppermute(own_tile, "strip", [(s, strips - 1 - s) for s in range(strips)])
    if date_count == MINI:
        slots, stack, freq = owner_table, None, center_freq
    else:
        slots = jnp.arange(MINI, dtype=jnp.int32)
        stack = [list(range(g, g + MINI)) for g in range(0, date_count, MINI)]
        freq = lax.dynamic_slice_in_dim(center_freq, position // MINI * MINI, MINI)
    tall = 2 * blocks * share
    height = tall * (cols // LANES + 1)
    tile = (MINI, LANES)
    coefs, taps, slot_marks, shift_marks, packed = pl.pallas_call(
        prep_kernel,
        out_shape=(
            jax.ShapeDtypeStruct((2 * ROUNDS * REACH,) + tile, jnp.float32),
            jax.ShapeDtypeStruct((TAPS,) + tile, jnp.float32),
            jax.ShapeDtypeStruct((MINI,) + tile, jnp.int32),
            jax.ShapeDtypeStruct((blocks + 1,) + tile, jnp.int32),
            jax.ShapeDtypeStruct((MINI, height, LANES), jnp.float32),
        ),
        in_specs=[hbm()] * 5,
        out_specs=(vmem(),) * 5,
        scratch_shapes=[
            pltpu.SMEM(freq.shape, jnp.float32),
            pltpu.SMEM(filter_taps.shape, jnp.float32),
            pltpu.SMEM(slots.shape, jnp.int32),
            pltpu.SMEM(coreg_shift.shape, jnp.int32),
            pltpu.VMEM(own_tile.shape, jnp.float32),
            pltpu.SemaphoreType.DMA((5,)),
        ],
        compiler_params=params(),
        name="prep",
    )(*(in_hbm(x) for x in (freq, filter_taps, slots, coreg_shift, own_tile)))
    packed = pl.pallas_call(
        rim_kernel,
        out_shape=jax.ShapeDtypeStruct(packed.shape, jnp.float32),
        in_specs=[pl.BlockSpec(memory_space=pltpu.SMEM)] + [vmem()] * 4,
        out_specs=vmem(),
        input_output_aliases={4: 0},
        compiler_params=params(),
        name="rim",
    )(lax.axis_index("strip")[None], slot_marks, shift_marks, other_tile, packed)
    data = lax.all_to_all(
        packed, "date", split_axis=0, concat_axis=0, axis_index_groups=stack, tiled=True
    )
    linked = pl.pallas_call(
        link_kernel,
        out_shape=jax.ShapeDtypeStruct((2, MINI, blocks * share // 2 * cols // 2), jnp.float32),
        in_specs=[vmem()] * 3,
        out_specs=vmem(),
        compiler_params=params(),
        name="link",
    )(taps, coefs, data.reshape(-1, LANES))
    if date_count == MINI:
        return linked
    date_ids = jnp.arange(date_count, dtype=jnp.int32)
    inverse = jnp.zeros((date_count,), jnp.int32).at[owner_table].set(date_ids)
    return to_owners(linked, inverse, blocks)


def solution(mesh):
    in_specs = (
        P(None, ("groups", "date"), None, "strip"),
        P(("groups", "date"), None),
        P("groups"),
        P(),
        P("groups"),
    )
    out_specs = P(None, "groups", ("date", "strip"))
    return jax.shard_map(shards, mesh=mesh, in_specs=in_specs, out_specs=out_specs, check_vma=False)
```

time: 21.6 us -> 18.9 us (0.87)
  blocking collectives: 0 us -> 14.7 us
  waiting for transfers between devices: 8.22 us -> 0.1 us
  starting transfers between devices: 7.77 us -> 0.49 us
  Pallas kernels: 4.4 us -> 3.42 us
  local copies, waits for them, and re-layouts: 0.92 us -> 0 us
    all_to_all x0 -> x1, blocking collectives: none -> 14.7 us  [shards(): lax.all_to_all(packed, 'date', split_axis=0, concat_axis=0, axis_index_gr...]
    all_to_all x1 -> x0, starting transfers between devices: 7.28 us -> none  [shards(): lax.all_to_all(packed, 'date', split_axis=0, concat_axis=0, axis_index_gr...]
    all_to_all x1 -> x0, waiting for transfers between devices: 7.02 us -> none  [shards(): lax.all_to_all(packed, 'date', split_axis=0, concat_axis=0, axis_index_gr...]
    ppermute x1, waiting for transfers between devices: 1.19 us -> 0.1 us  [shards(): lax.ppermute(own_tile, 'strip', [(s, strips - 1 - s) for s in range(strip...]
    pallas_call x3, Pallas kernels: 4.4 us -> 3.42 us  [the longest x1 1.83 us: shards(): pl.pallas_call(link_kernel, out_shape=jax.ShapeDtypeStruct((2, MINI, bloc...]
    unnamed x10 -> x0, local copies, waits for them, and re-layouts: 0.92 us -> none
  transfers between devices with their start and end apart: 2 -> 1, of which waited for: 2 -> 1; matrix products, arithmetic and copies ran while one was open for 0% -> 0% of each run, Pallas kernels for 3% -> 6%
where the time goes in v2:
time: 18.9 us; the launch traced here: 18.8 us
  blocking collectives  14.7 us (78%)
  Pallas kernels  3.42 us (18%)
  starting transfers between devices  0.49 us (3%)
    all_to_all x1, blocking collectives, shards(): lax.all_to_all(packed, 'date', split_axis=0, concat_axis=0, axis_index_gr...  14.7 us
    pallas_call x1, Pallas kernels, shards(): pl.pallas_call(link_kernel, out_shape=jax.ShapeDtypeStruct((2, MINI, bloc...  1.83 us
    pallas_call x1, Pallas kernels, shards(): pl.pallas_call(prep_kernel, out_shape=(jax.ShapeDtypeStruct((2 * ROUNDS *...  1.08 us
    pallas_call x1, Pallas kernels, shards(): pl.pallas_call(rim_kernel, out_shape=jax.ShapeDtypeStruct(packed.shape, j...  0.51 us
    ppermute x1, starting transfers between devices, shards(): lax.ppermute(own_tile, 'strip', [(s, strips - 1 - s) for s in range(strip...  0.49 us
  transfers between devices with their start and end apart: 1, of which 1 were waited for; matrix products, arithmetic and copies ran while one was open for 0% of the time, Pallas kernels for 6%

profile of v2, /device:TPU:0, one launch (start us, length us, event | category | flops | bytes accessed | tf_op | source)
XLA Modules:
  0.0 18.8 jit_solution(2569110128810097126)
XLA Ops:
  0.0 0.5 %collective-permute-start = (f32[2,32,512]{2,1,0:T(8,128)}, f32[2,32,512]{2,1,0:T(8,128)S(1)}, u32[]{:S(2)}, u32[]{:S(2)}) collective-permute-start(f32[2,32,512]{2,1,0:T(8,128)} %bitcast.4), channel_id=1, source_target_pairs={{0,1},{1,0},{2,3},{3,2},{4,5},{5,4},{6,7},{7,6},{8,9},{9,8},{10,11... | collective-permute-start | bytes 393224 | tf_op jit(solution)/shard_map/ppermute | solution.py:252
  0.5 1.1 %prep.1 = (f32[48,8,128]{2,1,0:T(8,128)S(1)}, f32[17,8,128]{2,1,0:T(8,128)S(1)}, s32[8,8,128]{2,1,0:T(8,128)S(1)}, s32[3,8,128]{2,1,0:T(8,128)S(1)}, f32[8,40,128]{2,1,0:T(8,128)S(1)}) custom-call(f32[8]{0:T(128)} %freq_hbm.1, f32[17]{0:T(128)} %tap_hbm.1, s32[8]{0:T(128)} %slot_hbm.1, s32[1,2]{1,0:T(1,128)} %shift_hbm.1, f32[2,32,512]{2,1,0:T(8,128)} %bitcast.5), custom_call_target="tpu_custom_call" | custom-call | tf_op jit(solution)/shard_map/prep/pallas_call | solution.py:262
  1.6 0.1 collective-permute-done.other_ref
  1.7 0.5 %rim.1 = f32[8,40,128]{2,1,0:T(8,128)S(1)} custom-call(s32[1]{0:T(128)} %bitcast.1.place_ref, s32[8,8,128]{2,1,0:T(8,128)S(1)} %get-tuple-element.12.slot_ref, s32[3,8,128]{2,1,0:T(8,128)S(1)} %get-tuple-element.13.shift_ref, f32[2,32,512]{2,1,0:T(8,128)S(1)} %collective-permute-done.other_ref, ...), custom_call_target="tpu_custom_call", output_to_operand_aliasing={{}: (4, {})} | custom-call | tf_op jit(solution)/shard_map/rim/pallas_call | solution.py:284
  2.2 14.7 %all_to_all.5 = f32[8,40,128]{2,1,0:T(8,128)S(1)} all-to-all(f32[8,40,128]{2,1,0:T(8,128)S(1)} %rim.1), channel_id=1, replica_groups=mesh['groups'=2,'date'=8,'strip'=2] {'date'}, dimensions={0} | all-to-all | bytes 327680 | tf_op jit(solution)/shard_map/all_to_all | solution.py:293
  16.9 1.8 %link.1 = f32[2,8,512]{2,1,0:T(8,128)} custom-call(f32[17,8,128]{2,1,0:T(8,128)S(1)} %get-tuple-element.10.tap_ref, f32[48,8,128]{2,1,0:T(8,128)S(1)} %get-tuple-element.11.coef_ref, f32[320,128]{1,0:T(8,128)S(1)} %bitcast.3), custom_call_target="tpu_custom_call" | custom-call | tf_op jit(solution)/shard_map/link/pallas_call | solution.py:296
Async XLA Ops:
  0.0 1.7 %collective-permute-start = (f32[2,32,512]{2,1,0:T(8,128)}, f32[2,32,512]{2,1,0:T(8,128)S(1)}, u32[]{:S(2)}, u32[]{:S(2)}) collective-permute-start(f32[2,32,512]{2,1,0:T(8,128)} %bitcast.4), channel_id=1, source_target_pairs={{0,1},{1,0},{2,3},{3,2},{4,5},{5,4},{6,7},{7,6},{8,9},{9,8},{10,11... | collective-permute-start | bytes 393224 | tf_op jit(solution)/shard_map/ppermute | solution.py:252

commit v3 on v2

--- a/solution.py
+++ b/solution.py
@@ -12,6 +12,7 @@
 ITERS = 3
 LANES = 128
 REACH = TAPS // 2
+ORDER = (4, 7, 5, 6, 0, 2, 1, 3)
 VMEM_LIMIT = 16 * 1024 * 1024
 
 
@@ -54,6 +55,12 @@
     lane = lax.broadcasted_iota(jnp.int32, (MINI, LANES), 1)
     for copy in copies[:4]:
         copy.wait()
+    slots = []
+    for q in range(MINI):
+        slot = jnp.int32(0)
+        for place, member in enumerate(ORDER):
+            slot = jnp.where(slot_ref[q] == member, place, slot)
+        slots.append(slot)
 
     def freq_of(index):
         total = jnp.zeros((MINI, LANES), jnp.float32)
@@ -74,7 +81,7 @@
     for t in range(TAPS):
         tap_out[t] = jnp.full((MINI, LANES), tap_ref[t], jnp.float32)
     for q in range(MINI):
-        slot_out[q] = jnp.full((MINI, LANES), slot_ref[q], jnp.int32)
+        slot_out[q] = jnp.full((MINI, LANES), slots[q], jnp.int32)
     _, rows, cols = tile_ref.shape
     blocks = shift_ref.shape[1]
     block_rows = rows // blocks
@@ -97,17 +104,17 @@
             for q in range(MINI):
                 for b in range(packed_ref.shape[1] // height):
                     at = b * height + (c * blocks + e) * share
-                    packed_ref[slot_ref[q], at : at + share, :] = moved[
+                    packed_ref[slots[q], at : at + share, :] = moved[
                         q * share : (q + 1) * share, b * LANES : (b + 1) * LANES
                     ]
 
 
-def rim_kernel(place_ref, slot_ref, shift_ref, other_ref, packed_ref, out_ref):
+def rim_kernel(slot_ref, shift_ref, other_ref, packed_ref, out_ref):
     _, rows, cols = other_ref.shape
     blocks = shift_ref.shape[0] - 1
     block_rows = rows // blocks
     share = block_rows // MINI
-    first = place_ref[0] == 0
+    first = lax.axis_index("strip") == 0
     lane = lax.broadcasted_iota(jnp.int32, (MINI, LANES), 1)
     reach = SMAX + REACH
     moved = []
@@ -115,10 +122,8 @@
         for e in range(blocks):
             lines = pl.ds(e * block_rows, block_rows)
             rim = jnp.where(first, other_ref[c, lines, 0:LANES], other_ref[c, lines, cols - LANES : cols])
-            shift = jnp.concatenate([shift_ref[e]] * (block_rows // MINI), axis=0)
-            for bit in range((2 * SMAX).bit_length()):
-                rim = jnp.where(shift & (1 << bit) != 0, pltpu.roll(rim, LANES - (1 << bit), 1), rim)
-            moved.append(pltpu.roll(rim, reach, 1))
+            source = jnp.concatenate([(lane - reach + shift_ref[e]) & (LANES - 1)] * (block_rows // MINI), axis=0)
+            moved.append(jnp.take_along_axis(rim, source, axis=1))
     pieces = [
         jnp.concatenate([m[q * share : (q + 1) * share] for m in moved], axis=0) for q in range(MINI)
     ]
@@ -160,15 +165,22 @@
     target = lax.broadcasted_iota(jnp.int32, (2 * LANES, LANES), 1)
     weights = jnp.where(source // 2 == target, 0.25, 0.0).astype(jnp.bfloat16)
 
+    date = lax.broadcasted_iota(jnp.int32, (MINI, LANES), 0)
+    place_of = jnp.zeros((MINI, LANES), jnp.int32)
+    for place, member in enumerate(ORDER):
+        place_of = jnp.where(date == member, place, place_of)
+
+    def load(row):
+        arrived = data_ref[pl.ds(row, MINI, stride=stride), :]
+        return jnp.take_along_axis(arrived, place_of, axis=0)
+
     def sums_of(e, b):
         sums = [None] * fields
         for p in range(2):
             pieces = []
             for c in range(2):
                 row = (c * blocks + e) * 2 + p
-                pieces.append(
-                    [data_ref[pl.ds((b + i) * height + row, MINI, stride=stride), :] for i in range(2)]
-                )
+                pieces.append([load((b + i) * height + row) for i in range(2)])
 
             def at(c, t):
                 here, there = pieces[c]
@@ -251,10 +263,9 @@
     position = lax.axis_index("date")
     other_tile = lax.ppermute(own_tile, "strip", [(s, strips - 1 - s) for s in range(strips)])
     if date_count == MINI:
-        slots, stack, freq = owner_table, None, center_freq
+        slots, freq = owner_table, center_freq
     else:
         slots = jnp.arange(MINI, dtype=jnp.int32)
-        stack = [list(range(g, g + MINI)) for g in range(0, date_count, MINI)]
         freq = lax.dynamic_slice_in_dim(center_freq, position // MINI * MINI, MINI)
     tall = 2 * blocks * share
     height = tall * (cols // LANES + 1)
@@ -284,14 +295,15 @@
     packed = pl.pallas_call(
         rim_kernel,
         out_shape=jax.ShapeDtypeStruct(packed.shape, jnp.float32),
-        in_specs=[pl.BlockSpec(memory_space=pltpu.SMEM)] + [vmem()] * 4,
+        in_specs=[vmem()] * 4,
         out_specs=vmem(),
-        input_output_aliases={4: 0},
+        input_output_aliases={3: 0},
         compiler_params=params(),
         name="rim",
-    )(lax.axis_index("strip")[None], slot_marks, shift_marks, other_tile, packed)
+    )(slot_marks, shift_marks, other_tile, packed)
+    stacks = [[g + member for member in ORDER] for g in range(0, date_count, MINI)]
     data = lax.all_to_all(
-        packed, "date", split_axis=0, concat_axis=0, axis_index_groups=stack, tiled=True
+        packed, "date", split_axis=0, concat_axis=0, axis_index_groups=stacks, tiled=True
     )
     linked = pl.pallas_call(
         link_kernel,

time: 18.9 us -> 16.1 us (0.85)
  blocking collectives: 14.7 us -> 12.3 us
  Pallas kernels: 3.42 us -> 3.04 us
    all_to_all x1, blocking collectives: 14.7 us -> 12.3 us  [shards(): lax.all_to_all(packed, 'date', split_axis=0, concat_axis=0, axis_index_gr...]
    pallas_call x1, Pallas kernels: 0.51 us -> 0.11 us  [shards(): pl.pallas_call(rim_kernel, out_shape=jax.ShapeDtypeStruct(packed.shape, j...]
  transfers between devices with their start and end apart: 1 -> 1, of which waited for: 1 -> 1; matrix products, arithmetic and copies ran while one was open for 0% -> 0% of each run, Pallas kernels for 6% -> 7%
where the time goes in v3:
time: 16.1 us; the launch traced here: 15.9 us
  blocking collectives  12.3 us (76%)
  Pallas kernels  3.04 us (19%)
  starting transfers between devices  0.49 us (3%)
    all_to_all x1, blocking collectives, shards(): lax.all_to_all(packed, 'date', split_axis=0, concat_axis=0, axis_index_gr...  12.3 us
    pallas_call x1, Pallas kernels, shards(): pl.pallas_call(link_kernel, out_shape=jax.ShapeDtypeStruct((2, MINI, bloc...  1.85 us
    pallas_call x1, Pallas kernels, shards(): pl.pallas_call(prep_kernel, out_shape=(jax.ShapeDtypeStruct((2 * ROUNDS *...  1.08 us
    ppermute x1, starting transfers between devices, shards(): lax.ppermute(own_tile, 'strip', [(s, strips - 1 - s) for s in range(strip...  0.49 us
  transfers between devices with their start and end apart: 1, of which 1 were waited for; matrix products, arithmetic and copies ran while one was open for 0% of the time, Pallas kernels for 7%

profile of v3, /device:TPU:0, one launch (start us, length us, event | category | flops | bytes accessed | tf_op | source)
XLA Modules:
  0.0 15.9 jit_solution(16748719016083767385)
XLA Ops:
  0.0 0.5 %collective-permute-start = (f32[2,32,512]{2,1,0:T(8,128)}, f32[2,32,512]{2,1,0:T(8,128)S(1)}, u32[]{:S(2)}, u32[]{:S(2)}) collective-permute-start(f32[2,32,512]{2,1,0:T(8,128)} %bitcast.3), channel_id=1, source_target_pairs={{0,1},{1,0},{2,3},{3,2},{4,5},{5,4},{6,7},{7,6},{8,9},{9,8},{10,11... | collective-permute-start | bytes 393224 | tf_op jit(solution)/shard_map/ppermute | solution.py:264
  0.5 1.1 %prep.1 = (f32[48,8,128]{2,1,0:T(8,128)S(1)}, f32[17,8,128]{2,1,0:T(8,128)S(1)}, s32[8,8,128]{2,1,0:T(8,128)S(1)}, s32[3,8,128]{2,1,0:T(8,128)S(1)}, f32[8,40,128]{2,1,0:T(8,128)S(1)}) custom-call(f32[8]{0:T(128)} %freq_hbm.1, f32[17]{0:T(128)} %tap_hbm.1, s32[8]{0:T(128)} %slot_hbm.1, s32[1,2]{1,0:T(1,128)} %shift_hbm.1, f32[2,32,512]{2,1,0:T(8,128)} %bitcast.4), custom_call_target="tpu_custom_call" | custom-call | tf_op jit(solution)/shard_map/prep/pallas_call | solution.py:273
  1.6 0.1 collective-permute-done.other_ref
  1.7 0.1 rim.1
  1.8 12.3 %all_to_all.5 = f32[8,40,128]{2,1,0:T(8,128)S(1)} all-to-all(f32[8,40,128]{2,1,0:T(8,128)S(1)} %rim.1), channel_id=1, replica_groups={{8,14,10,12,0,4,2,6},{9,15,11,13,1,5,3,7},{24,30,26,28,16,20,18,22},{25..., dimensions={0} | all-to-all | bytes 327680 | tf_op jit(solution)/shard_map/all_to_all | solution.py:305
  14.1 1.9 %link.1 = f32[2,8,512]{2,1,0:T(8,128)} custom-call(f32[17,8,128]{2,1,0:T(8,128)S(1)} %get-tuple-element.10.tap_ref, f32[48,8,128]{2,1,0:T(8,128)S(1)} %get-tuple-element.11.coef_ref, f32[320,128]{1,0:T(8,128)S(1)} %bitcast.2), custom_call_target="tpu_custom_call" | custom-call | tf_op jit(solution)/shard_map/link/pallas_call | solution.py:308
Async XLA Ops:
  0.0 1.7 %collective-permute-start = (f32[2,32,512]{2,1,0:T(8,128)}, f32[2,32,512]{2,1,0:T(8,128)S(1)}, u32[]{:S(2)}, u32[]{:S(2)}) collective-permute-start(f32[2,32,512]{2,1,0:T(8,128)} %bitcast.3), channel_id=1, source_target_pairs={{0,1},{1,0},{2,3},{3,2},{4,5},{5,4},{6,7},{7,6},{8,9},{9,8},{10,11... | collective-permute-start | bytes 393224 | tf_op jit(solution)/shard_map/ppermute | solution.py:264

commit v4 on v3

--- a/solution.py
+++ b/solution.py
@@ -12,7 +12,7 @@
 ITERS = 3
 LANES = 128
 REACH = TAPS // 2
-ORDER = (4, 7, 5, 6, 0, 2, 1, 3)
+ORDER = (5, 7, 3, 4, 0, 6, 1, 2)
 VMEM_LIMIT = 16 * 1024 * 1024
 
 
@@ -75,11 +75,14 @@
         rotation = jnp.where(lane // REACH == r, q, rotation)
     angle = rotation * (lane % REACH + 1).astype(jnp.float32)
     cosine, sine = jnp.cos(angle), jnp.sin(angle)
+    taps = [jnp.full((MINI, LANES), tap_ref[t], jnp.float32) for t in range(TAPS)]
     for j in range(ROUNDS * REACH):
-        coef_ref[2 * j] = jnp.broadcast_to(cosine[:, j : j + 1], (MINI, LANES))
-        coef_ref[2 * j + 1] = jnp.broadcast_to(sine[:, j : j + 1], (MINI, LANES))
-    for t in range(TAPS):
-        tap_out[t] = jnp.full((MINI, LANES), tap_ref[t], jnp.float32)
+        tap = taps[REACH + 1 + j % REACH]
+        coef_ref[2 * j] = tap * jnp.broadcast_to(cosine[:, j : j + 1], (MINI, LANES))
+        coef_ref[2 * j + 1] = tap * jnp.broadcast_to(sine[:, j : j + 1], (MINI, LANES))
+    tap_out[0] = taps[REACH]
+    for k in range(1, REACH + 1):
+        tap_out[k] = taps[REACH - k] / taps[REACH + k]
     for q in range(MINI):
         slot_out[q] = jnp.full((MINI, LANES), slots[q], jnp.int32)
     _, rows, cols = tile_ref.shape
@@ -160,22 +163,18 @@
     height = 4 * blocks
     stride = (nb + 1) * height
     lane = lax.broadcasted_iota(jnp.int32, (MINI, LANES), 1)
-    fields = 2 * ROUNDS + 1
-    source = lax.broadcasted_iota(jnp.int32, (2 * LANES, LANES), 0)
-    target = lax.broadcasted_iota(jnp.int32, (2 * LANES, LANES), 1)
-    weights = jnp.where(source // 2 == target, 0.25, 0.0).astype(jnp.bfloat16)
-
     date = lax.broadcasted_iota(jnp.int32, (MINI, LANES), 0)
     place_of = jnp.zeros((MINI, LANES), jnp.int32)
     for place, member in enumerate(ORDER):
         place_of = jnp.where(date == member, place, place_of)
+    even_lane = 2 * lane % LANES
 
     def load(row):
         arrived = data_ref[pl.ds(row, MINI, stride=stride), :]
         return jnp.take_along_axis(arrived, place_of, axis=0)
 
     def sums_of(e, b):
-        sums = [None] * fields
+        sums = None
         for p in range(2):
             pieces = []
             for c in range(2):
@@ -189,10 +188,10 @@
                 return pltpu.roll(jnp.where(lane < t, there, here), LANES - t, 1)
 
             centre = [at(c, REACH) for c in range(2)]
-            acc = [[tap_ref[REACH] * centre[c] for c in range(2)] for _ in range(ROUNDS)]
+            acc = [[tap_ref[0] * centre[c] for c in range(2)] for _ in range(ROUNDS)]
             for k in range(1, REACH + 1):
-                plus = [tap_ref[REACH + k] * at(c, REACH + k) for c in range(2)]
-                minus = [tap_ref[REACH - k] * at(c, REACH - k) for c in range(2)]
+                plus = [at(c, REACH + k) for c in range(2)]
+                minus = [tap_ref[k] * at(c, REACH - k) for c in range(2)]
                 even = [plus[c] + minus[c] for c in range(2)]
                 odd = [plus[c] - minus[c] for c in range(2)]
                 for r in range(ROUNDS):
@@ -207,34 +206,46 @@
                 terms.append(y_re * z_re + y_im * z_im)
                 terms.append(y_im * z_re - y_re * z_im)
             terms.append(centre[0] * centre[0] + centre[1] * centre[1])
-            sums = [t if s is None else s + t for s, t in zip(sums, terms)]
-        return jnp.concatenate(sums, axis=0)
+            sums = terms if sums is None else [s + t for s, t in zip(sums, terms)]
+        return sums
+
+    source = lax.broadcasted_iota(jnp.int32, (2 * LANES, LANES), 0)
+    target = lax.broadcasted_iota(jnp.int32, (2 * LANES, LANES), 1)
+    weights = jnp.where(source // 2 == target, 0.25, 0.0).astype(jnp.bfloat16)
+
+    def energy_of(re, im):
+        return jnp.sum(re * re + im * im, axis=0, keepdims=True)
+
+    def shrink(length):
+        return 1.0 / jnp.maximum(length, 1.0)
 
     for g in range(blocks * nb // 2):
         e, b = g // (nb // 2), g % (nb // 2) * 2
-        value = jnp.concatenate([sums_of(e, b), sums_of(e, b + 1)], axis=1)
-        looked = jnp.zeros((value.shape[0], LANES), jnp.float32)
-        for _ in range(3):
+        value = jnp.concatenate([jnp.concatenate(sums_of(e, b + i), axis=0) for i in range(2)], axis=1)
+        total = jnp.zeros((value.shape[0], LANES), jnp.float32)
+        for _ in range(2):
             part = value.astype(jnp.bfloat16)
             value = value - part.astype(jnp.float32)
-            looked = looked + jnp.dot(part, weights, preferred_element_type=jnp.float32)
-        field = [looked[f * MINI : (f + 1) * MINI] for f in range(fields)]
-        vec_re = jnp.ones((MINI, LANES), jnp.float32)
-        vec_im = jnp.zeros((MINI, LANES), jnp.float32)
-        for _ in range(ITERS):
+            total = total + jnp.dot(part, weights, preferred_element_type=jnp.float32)
+        field = [total[f * MINI : (f + 1) * MINI] for f in range(2 * ROUNDS + 1)]
+        vec_re = field[-1] + (field[0] + field[2] + field[4])
+        vec_im = field[1] + field[3] + field[5]
+        energies = [energy_of(vec_re, vec_im)]
+        for _ in range(1, ITERS):
             next_re = field[-1] * vec_re
             next_im = field[-1] * vec_im
             for r in range(ROUNDS):
                 o_re, o_im = partner(vec_re, 1 << r), partner(vec_im, 1 << r)
                 t_re, t_im = field[2 * r], field[2 * r + 1]
-                next_re = next_re + t_re * o_re - t_im * o_im
-                next_im = next_im + t_re * o_im + t_im * o_re
-            energy = jnp.sum(next_re * next_re + next_im * next_im, axis=0, keepdims=True)
-            factor = 1.0 / jnp.maximum(jnp.sqrt(energy), 1.0)
-            vec_re = next_re * factor
-            vec_im = next_im * factor
-        out_ref[0, :, pl.ds(g * LANES, LANES)] = vec_re
-        out_ref[1, :, pl.ds(g * LANES, LANES)] = vec_im
+                next_re = next_re + (t_re * o_re - t_im * o_im)
+                next_im = next_im + (t_re * o_im + t_im * o_re)
+            vec_re, vec_im = next_re, next_im
+            energies.append(energy_of(vec_re, vec_im))
+        factor = 1.0
+        for energy in energies:
+            factor = factor * shrink(jnp.sqrt(energy) * factor)
+        out_ref[0, :, pl.ds(g * LANES, LANES)] = vec_re * factor
+        out_ref[1, :, pl.ds(g * LANES, LANES)] = vec_im * factor
 
 
 def to_owners(linked, inverse, blocks):
@@ -274,7 +285,7 @@
         prep_kernel,
         out_shape=(
             jax.ShapeDtypeStruct((2 * ROUNDS * REACH,) + tile, jnp.float32),
-            jax.ShapeDtypeStruct((TAPS,) + tile, jnp.float32),
+            jax.ShapeDtypeStruct((REACH + 1,) + tile, jnp.float32),
             jax.ShapeDtypeStruct((MINI,) + tile, jnp.int32),
             jax.ShapeDtypeStruct((blocks + 1,) + tile, jnp.int32),
             jax.ShapeDtypeStruct((MINI, height, LANES), jnp.float32),

time: 16.1 us -> 15.1 us (0.938)
  blocking collectives: 12.3 us -> 11.4 us
    all_to_all x1, blocking collectives: 12.3 us -> 11.4 us  [shards(): lax.all_to_all(packed, 'date', split_axis=0, concat_axis=0, axis_index_gr...]
where the time goes in v4:
time: 15.1 us; the launch traced here: 14.9 us
  blocking collectives  11.4 us (75%)
  Pallas kernels  2.88 us (19%)
  starting transfers between devices  0.49 us (3%)
    all_to_all x1, blocking collectives, shards(): lax.all_to_all(packed, 'date', split_axis=0, concat_axis=0, axis_index_gr...  11.4 us
    pallas_call x1, Pallas kernels, shards(): pl.pallas_call(link_kernel, out_shape=jax.ShapeDtypeStruct((2, MINI, bloc...  1.69 us
    pallas_call x1, Pallas kernels, shards(): pl.pallas_call(prep_kernel, out_shape=(jax.ShapeDtypeStruct((2 * ROUNDS *...  1.08 us
    ppermute x1, starting transfers between devices, shards(): lax.ppermute(own_tile, 'strip', [(s, strips - 1 - s) for s in range(strip...  0.49 us
  transfers between devices with their start and end apart: 1, of which 1 were waited for; matrix products, arithmetic and copies ran while one was open for 0% of the time, Pallas kernels for 7%

profile of v4, /device:TPU:0, one launch (start us, length us, event | category | flops | bytes accessed | tf_op | source)
XLA Modules:
  0.0 14.9 jit_solution(10524342363847888850)
XLA Ops:
  0.0 0.5 %collective-permute-start = (f32[2,32,512]{2,1,0:T(8,128)}, f32[2,32,512]{2,1,0:T(8,128)S(1)}, u32[]{:S(2)}, u32[]{:S(2)}) collective-permute-start(f32[2,32,512]{2,1,0:T(8,128)} %bitcast.3), channel_id=1, source_target_pairs={{0,1},{1,0},{2,3},{3,2},{4,5},{5,4},{6,7},{7,6},{8,9},{9,8},{10,11... | collective-permute-start | bytes 393224 | tf_op jit(solution)/shard_map/ppermute | solution.py:275
  0.5 1.1 %prep.1 = (f32[48,8,128]{2,1,0:T(8,128)S(1)}, f32[9,8,128]{2,1,0:T(8,128)S(1)}, s32[8,8,128]{2,1,0:T(8,128)S(1)}, s32[3,8,128]{2,1,0:T(8,128)S(1)}, f32[8,40,128]{2,1,0:T(8,128)S(1)}) custom-call(f32[8]{0:T(128)} %freq_hbm.1, f32[17]{0:T(128)} %tap_hbm.1, s32[8]{0:T(128)} %slot_hbm.1, s32[1,2]{1,0:T(1,128)} %shift_hbm.1, f32[2,32,512]{2,1,0:T(8,128)} %bitcast.4), custom_call_target="tpu_custom_call" | custom-call | tf_op jit(solution)/shard_map/prep/pallas_call | solution.py:284
  1.6 0.1 collective-permute-done.other_ref
  1.7 0.1 rim.1
  1.8 11.4 %all_to_all.5 = f32[8,40,128]{2,1,0:T(8,128)S(1)} all-to-all(f32[8,40,128]{2,1,0:T(8,128)S(1)} %rim.1), channel_id=1, replica_groups={{10,14,6,8,0,12,2,4},{11,15,7,9,1,13,3,5},{26,30,22,24,16,28,18,20},{27..., dimensions={0} | all-to-all | bytes 327680 | tf_op jit(solution)/shard_map/all_to_all | solution.py:316
  13.2 1.7 %link.1 = f32[2,8,512]{2,1,0:T(8,128)} custom-call(f32[9,8,128]{2,1,0:T(8,128)S(1)} %get-tuple-element.10.tap_ref, f32[48,8,128]{2,1,0:T(8,128)S(1)} %get-tuple-element.11.coef_ref, f32[320,128]{1,0:T(8,128)S(1)} %bitcast.2), custom_call_target="tpu_custom_call" | custom-call | tf_op jit(solution)/shard_map/link/pallas_call | solution.py:319
Async XLA Ops:
  0.0 1.7 %collective-permute-start = (f32[2,32,512]{2,1,0:T(8,128)}, f32[2,32,512]{2,1,0:T(8,128)S(1)}, u32[]{:S(2)}, u32[]{:S(2)}) collective-permute-start(f32[2,32,512]{2,1,0:T(8,128)} %bitcast.3), channel_id=1, source_target_pairs={{0,1},{1,0},{2,3},{3,2},{4,5},{5,4},{6,7},{7,6},{8,9},{9,8},{10,11... | collective-permute-start | bytes 393224 | tf_op jit(solution)/shard_map/ppermute | solution.py:275

commit v5 on v4

--- a/solution.py
+++ b/solution.py
@@ -30,6 +30,15 @@
 
 def params():
     return pltpu.CompilerParams(vmem_limit_bytes=VMEM_LIMIT)
+
+
+def sources(shift, lane, cols):
+    first = [LANES - REACH - SMAX + shift + 2 * lane + odd for odd in range(2)]
+    piece = [f >> (LANES.bit_length() - 1) for f in first]
+    count = cols // LANES
+    index = [2 * h + piece[odd] for odd in range(2) for h in range(count // 2)]
+    index.append(jnp.where(lane < LANES // 2, count + piece[0], count - 1 + piece[1]))
+    return [f & (LANES - 1) for f in first], index
 
 
 def prep_kernel(
@@ -96,20 +105,33 @@
         offsets = jnp.where(row // share % blocks == e, shift_ref[0, e] + SMAX, offsets)
         shift_out[e] = jnp.full((MINI, LANES), shift_ref[0, e] + SMAX, jnp.int32)
     shift_out[blocks] = offsets
+    count = cols // LANES
+    tall_lane = lax.broadcasted_iota(jnp.int32, (block_rows, LANES), 1)
+    plans = [sources(shift_ref[0, e] + SMAX, tall_lane, cols) for e in range(blocks)]
     copies[4].wait()
-    total = cols + 2 * LANES
     for e in range(blocks):
-        offset = LANES - REACH + shift_ref[0, e]
+        lanes, index = plans[e]
         for c in range(2):
-            rim = jnp.zeros((block_rows, LANES), jnp.float32)
-            lines = tile_ref[c, e * block_rows : (e + 1) * block_rows, :]
-            moved = pltpu.roll(jnp.concatenate([rim, lines, rim], axis=1), total - offset, 1)
-            for q in range(MINI):
-                for b in range(packed_ref.shape[1] // height):
-                    at = b * height + (c * blocks + e) * share
-                    packed_ref[slots[q], at : at + share, :] = moved[
-                        q * share : (q + 1) * share, b * LANES : (b + 1) * LANES
-                    ]
+            lines = pl.ds(e * block_rows, block_rows)
+            taken = [
+                [
+                    jnp.take_along_axis(tile_ref[c, lines, v * LANES : (v + 1) * LANES], lanes[odd], axis=1)
+                    for v in range(count)
+                ]
+                for odd in range(2)
+            ]
+            for b in range(count + 1):
+                value = jnp.zeros((block_rows, LANES), jnp.float32)
+                low = count if b == count else b % (count // 2) * 2
+                for v in range(max(low, 1), min(low + 3, count) + 1):
+                    if b == count:
+                        source = jnp.where(tall_lane < LANES // 2, taken[0][v - 1], taken[1][v - 1])
+                    else:
+                        source = taken[b // (count // 2)][v - 1]
+                    value = jnp.where(index[b] == v, source, value)
+                at = b * height + c * blocks * share + e * share
+                for q in range(MINI):
+                    packed_ref[slots[q], at : at + share, :] = value[q * share : (q + 1) * share]
 
 
 def rim_kernel(slot_ref, shift_ref, other_ref, packed_ref, out_ref):
@@ -117,34 +139,35 @@
     blocks = shift_ref.shape[0] - 1
     block_rows = rows // blocks
     share = block_rows // MINI
+    height = 2 * blocks * share
+    count = cols // LANES
     first = lax.axis_index("strip") == 0
     lane = lax.broadcasted_iota(jnp.int32, (MINI, LANES), 1)
-    reach = SMAX + REACH
+    tall_lane = lax.broadcasted_iota(jnp.int32, (block_rows, LANES), 1)
     moved = []
     for c in range(2):
         for e in range(blocks):
             lines = pl.ds(e * block_rows, block_rows)
             rim = jnp.where(first, other_ref[c, lines, 0:LANES], other_ref[c, lines, cols - LANES : cols])
-            source = jnp.concatenate([(lane - reach + shift_ref[e]) & (LANES - 1)] * (block_rows // MINI), axis=0)
-            moved.append(jnp.take_along_axis(rim, source, axis=1))
+            shift = jnp.concatenate([shift_ref[e]] * (block_rows // MINI), axis=0)
+            lanes, _ = sources(shift, tall_lane, cols)
+            moved.append([jnp.take_along_axis(rim, lanes[odd], axis=1) for odd in range(2)])
     pieces = [
-        jnp.concatenate([m[q * share : (q + 1) * share] for m in moved], axis=0) for q in range(MINI)
+        [jnp.concatenate([m[odd][q * share : (q + 1) * share] for m in moved], axis=0) for q in range(MINI)]
+        for odd in range(2)
     ]
-    edge = reach - shift_ref[blocks]
-    height = 2 * blocks * share
-    last = cols // LANES
-    side = jnp.where(first, 0, 1)
-    masks = {
-        0: lane + (1 - side) * 2 * LANES < edge,
-        last - 1: lane - side * 4 * LANES >= edge + LANES,
-        last: lane - side * 4 * LANES >= edge,
-    }
+    _, index = sources(shift_ref[blocks], lane, cols)
+    wanted = jnp.where(first, count + 1, 0)
+    masks = [piece == wanted for piece in index]
     for j in range(MINI):
-        rim = pieces[0]
+        rims = [pieces[odd][0] for odd in range(2)]
         for q in range(1, MINI):
-            rim = jnp.where(slot_ref[q] == j, pieces[q], rim)
-        for b, mask in masks.items():
+            hit = slot_ref[q] == j
+            rims = [jnp.where(hit, pieces[odd][q], rims[odd]) for odd in range(2)]
+        rims.append(jnp.where(lane < LANES // 2, rims[0], rims[1]))
+        for b, mask in enumerate(masks):
             at = slice(b * height, (b + 1) * height)
+            rim = rims[2 if b == count else b // (count // 2)]
             out_ref[j, at, :] = jnp.where(mask, rim, packed_ref[j, at, :])
 
 
@@ -173,45 +196,57 @@
         arrived = data_ref[pl.ds(row, MINI, stride=stride), :]
         return jnp.take_along_axis(arrived, place_of, axis=0)
 
-    def sums_of(e, b):
+    def sums_of(e, h):
         sums = None
         for p in range(2):
             pieces = []
             for c in range(2):
                 row = (c * blocks + e) * 2 + p
-                pieces.append([load((b + i) * height + row) for i in range(2)])
-
-            def at(c, t):
-                here, there = pieces[c]
-                if t == 0:
-                    return here
-                return pltpu.roll(jnp.where(lane < t, there, here), LANES - t, 1)
-
-            centre = [at(c, REACH) for c in range(2)]
-            acc = [[tap_ref[0] * centre[c] for c in range(2)] for _ in range(ROUNDS)]
+                tail = load(nb * height + row)
+                for odd in range(2):
+                    block = odd * (nb // 2) + h
+                    if h + 1 < nb // 2:
+                        there = load((block + 1) * height + row)
+                    else:
+                        there = pltpu.roll(tail, LANES // 2, 1) if odd else tail
+                    pieces.append((load(block * height + row), there))
+            cache = {}
+
+            def at(c, l):
+                m, odd = l // 2, l % 2
+                if (c, l) not in cache:
+                    here, there = pieces[2 * c + odd]
+                    if m:
+                        here = pltpu.roll(jnp.where(lane < m, there, here), LANES - m, 1)
+                    cache[c, l] = here
+                return cache[c, l]
+
+            centre = [[at(c, REACH + odd) for c in range(2)] for odd in range(2)]
+            acc = [
+                [[tap_ref[0] * centre[odd][c] for c in range(2)] for _ in range(ROUNDS)] for odd in range(2)
+            ]
             for k in range(1, REACH + 1):
-                plus = [at(c, REACH + k) for c in range(2)]
-                minus = [tap_ref[k] * at(c, REACH - k) for c in range(2)]
-                even = [plus[c] + minus[c] for c in range(2)]
-                odd = [plus[c] - minus[c] for c in range(2)]
+                for odd in range(2):
+                    plus = [at(c, REACH + odd + k) for c in range(2)]
+                    minus = [tap_ref[k] * at(c, REACH + odd - k) for c in range(2)]
+                    even = [plus[c] + minus[c] for c in range(2)]
+                    diff = [plus[c] - minus[c] for c in range(2)]
+                    for r in range(ROUNDS):
+                        j = r * REACH + k - 1
+                        cosine, sine = coef_ref[2 * j], coef_ref[2 * j + 1]
+                        total = acc[odd][r]
+                        total[0] = total[0] + (cosine * even[0] - sine * diff[1])
+                        total[1] = total[1] + (cosine * even[1] + sine * diff[0])
+            for odd in range(2):
+                terms = []
                 for r in range(ROUNDS):
-                    j = r * REACH + k - 1
-                    cosine, sine = coef_ref[2 * j], coef_ref[2 * j + 1]
-                    acc[r][0] = acc[r][0] + (cosine * even[0] - sine * odd[1])
-                    acc[r][1] = acc[r][1] + (cosine * even[1] + sine * odd[0])
-            terms = []
-            for r in range(ROUNDS):
-                y_re, y_im = acc[r]
-                z_re, z_im = partner(y_re, 1 << r), partner(y_im, 1 << r)
-                terms.append(y_re * z_re + y_im * z_im)
-                terms.append(y_im * z_re - y_re * z_im)
-            terms.append(centre[0] * centre[0] + centre[1] * centre[1])
-            sums = terms if sums is None else [s + t for s, t in zip(sums, terms)]
+                    y_re, y_im = acc[odd][r]
+                    z_re, z_im = partner(y_re, 1 << r), partner(y_im, 1 << r)
+                    terms.append(y_re * z_re + y_im * z_im)
+                    terms.append(y_im * z_re - y_re * z_im)
+                terms.append(centre[odd][0] * centre[odd][0] + centre[odd][1] * centre[odd][1])
+                sums = terms if sums is None else [s + t for s, t in zip(sums, terms)]
         return sums
-
-    source = lax.broadcasted_iota(jnp.int32, (2 * LANES, LANES), 0)
-    target = lax.broadcasted_iota(jnp.int32, (2 * LANES, LANES), 1)
-    weights = jnp.where(source // 2 == target, 0.25, 0.0).astype(jnp.bfloat16)
 
     def energy_of(re, im):
         return jnp.sum(re * re + im * im, axis=0, keepdims=True)
@@ -220,14 +255,7 @@
         return 1.0 / jnp.maximum(length, 1.0)
 
     for g in range(blocks * nb // 2):
-        e, b = g // (nb // 2), g % (nb // 2) * 2
-        value = jnp.concatenate([jnp.concatenate(sums_of(e, b + i), axis=0) for i in range(2)], axis=1)
-        total = jnp.zeros((value.shape[0], LANES), jnp.float32)
-        for _ in range(2):
-            part = value.astype(jnp.bfloat16)
-            value = value - part.astype(jnp.float32)
-            total = total + jnp.dot(part, weights, preferred_element_type=jnp.float32)
-        field = [total[f * MINI : (f + 1) * MINI] for f in range(2 * ROUNDS + 1)]
+        field = [total * 0.25 for total in sums_of(g // (nb // 2), g % (nb // 2))]
         vec_re = field[-1] + (field[0] + field[2] + field[4])
         vec_im = field[1] + field[3] + field[5]
         energies = [energy_of(vec_re, vec_im)]

time: 15.1 us -> 14.9 us (0.987)
    pallas_call x1, Pallas kernels: 1.69 us -> 1.49 us  [shards(): pl.pallas_call(link_kernel, out_shape=jax.ShapeDtypeStruct((2, MINI, bloc...]
  transfers between devices with their start and end apart: 1 -> 1, of which waited for: 1 -> 1; matrix products, arithmetic and copies ran while one was open for 0% -> 0% of each run, Pallas kernels for 7% -> 8%
where the time goes in v5:
time: 14.9 us; the launch traced here: 14.7 us
  blocking collectives  11.4 us (77%)
  Pallas kernels  2.76 us (19%)
  starting transfers between devices  0.49 us (3%)
    all_to_all x1, blocking collectives, shards(): lax.all_to_all(packed, 'date', split_axis=0, concat_axis=0, axis_index_gr...  11.4 us
    pallas_call x1, Pallas kernels, shards(): pl.pallas_call(link_kernel, out_shape=jax.ShapeDtypeStruct((2, MINI, bloc...  1.49 us
    pallas_call x1, Pallas kernels, shards(): pl.pallas_call(prep_kernel, out_shape=(jax.ShapeDtypeStruct((2 * ROUNDS *...  1.13 us
    ppermute x1, starting transfers between devices, shards(): lax.ppermute(own_tile, 'strip', [(s, strips - 1 - s) for s in range(strip...  0.49 us
  transfers between devices with their start and end apart: 1, of which 1 were waited for; matrix products, arithmetic and copies ran while one was open for 0% of the time, Pallas kernels for 8%

profile of v5, /device:TPU:0, one launch (start us, length us, event | category | flops | bytes accessed | tf_op | source)
XLA Modules:
  0.0 14.7 jit_solution(5147314791521779779)
XLA Ops:
  0.0 0.5 %collective-permute-start = (f32[2,32,512]{2,1,0:T(8,128)}, f32[2,32,512]{2,1,0:T(8,128)S(1)}, u32[]{:S(2)}, u32[]{:S(2)}) collective-permute-start(f32[2,32,512]{2,1,0:T(8,128)} %bitcast.3), channel_id=1, source_target_pairs={{0,1},{1,0},{2,3},{3,2},{4,5},{5,4},{6,7},{7,6},{8,9},{9,8},{10,11... | collective-permute-start | bytes 393224 | tf_op jit(solution)/shard_map/ppermute | solution.py:303
  0.5 1.1 %prep.1 = (f32[48,8,128]{2,1,0:T(8,128)S(1)}, f32[9,8,128]{2,1,0:T(8,128)S(1)}, s32[8,8,128]{2,1,0:T(8,128)S(1)}, s32[3,8,128]{2,1,0:T(8,128)S(1)}, f32[8,40,128]{2,1,0:T(8,128)S(1)}) custom-call(f32[8]{0:T(128)} %freq_hbm.1, f32[17]{0:T(128)} %tap_hbm.1, s32[8]{0:T(128)} %slot_hbm.1, s32[1,2]{1,0:T(1,128)} %shift_hbm.1, f32[2,32,512]{2,1,0:T(8,128)} %bitcast.4), custom_call_target="tpu_custom_call" | custom-call | tf_op jit(solution)/shard_map/prep/pallas_call | solution.py:312
  1.6 0.1 collective-permute-done.other_ref
  1.7 0.1 rim.1
  1.8 11.4 %all_to_all.5 = f32[8,40,128]{2,1,0:T(8,128)S(1)} all-to-all(f32[8,40,128]{2,1,0:T(8,128)S(1)} %rim.1), channel_id=1, replica_groups={{10,14,6,8,0,12,2,4},{11,15,7,9,1,13,3,5},{26,30,22,24,16,28,18,20},{27..., dimensions={0} | all-to-all | bytes 327680 | tf_op jit(solution)/shard_map/all_to_all | solution.py:344
  13.2 1.5 %link.1 = f32[2,8,512]{2,1,0:T(8,128)} custom-call(f32[9,8,128]{2,1,0:T(8,128)S(1)} %get-tuple-element.10.tap_ref, f32[48,8,128]{2,1,0:T(8,128)S(1)} %get-tuple-element.11.coef_ref, f32[320,128]{1,0:T(8,128)S(1)} %bitcast.2), custom_call_target="tpu_custom_call" | custom-call | tf_op jit(solution)/shard_map/link/pallas_call | solution.py:347
Async XLA Ops:
  0.0 1.7 %collective-permute-start = (f32[2,32,512]{2,1,0:T(8,128)}, f32[2,32,512]{2,1,0:T(8,128)S(1)}, u32[]{:S(2)}, u32[]{:S(2)}) collective-permute-start(f32[2,32,512]{2,1,0:T(8,128)} %bitcast.3), channel_id=1, source_target_pairs={{0,1},{1,0},{2,3},{3,2},{4,5},{5,4},{6,7},{7,6},{8,9},{9,8},{10,11... | collective-permute-start | bytes 393224 | tf_op jit(solution)/shard_map/ppermute | solution.py:303

commit v6 on v5

--- a/solution.py
+++ b/solution.py
@@ -13,6 +13,7 @@
 LANES = 128
 REACH = TAPS // 2
 ORDER = (5, 7, 3, 4, 0, 6, 1, 2)
+LANE_BITS = LANES.bit_length() - 1
 VMEM_LIMIT = 16 * 1024 * 1024
 
 
@@ -34,11 +35,24 @@
 
 def sources(shift, lane, cols):
     first = [LANES - REACH - SMAX + shift + 2 * lane + odd for odd in range(2)]
-    piece = [f >> (LANES.bit_length() - 1) for f in first]
+    piece = [lax.shift_right_logical(f, LANE_BITS) for f in first]
+    index = [2 * h + piece[odd] for odd in range(2) for h in range(cols // LANES // 2)]
+    return [f & (LANES - 1) for f in first], index
+
+
+def tails(lines_of, shift_of, wanted, lane, cols, blocks, share):
     count = cols // LANES
-    index = [2 * h + piece[odd] for odd in range(2) for h in range(count // 2)]
-    index.append(jnp.where(lane < LANES // 2, count + piece[0], count - 1 + piece[1]))
-    return [f & (LANES - 1) for f in first], index
+    row = lax.broadcasted_iota(jnp.int32, lane.shape, 0) % share
+    column = 2 * (lane % REACH) + lane // REACH % 2
+    total = jnp.zeros(lane.shape, jnp.float32)
+    for e in range(blocks):
+        first = LANES - REACH - SMAX + shift_of(e) + column
+        mine = count + lax.shift_right_logical(first, LANE_BITS) == wanted
+        for c in range(2):
+            taken = jnp.take_along_axis(lines_of(c, e), first & (LANES - 1), axis=1)
+            here = lane // (2 * REACH) == (c * blocks + e) * share + row
+            total = jnp.where(mine & here, taken, total)
+    return sum(pltpu.roll(total, (lane.shape[0] - p) % lane.shape[0], 0) if p else total for p in range(share))
 
 
 def prep_kernel(
@@ -98,7 +112,8 @@
     blocks = shift_ref.shape[1]
     block_rows = rows // blocks
     share = block_rows // MINI
-    height = 2 * blocks * share
+    tall = 2 * blocks * share
+    height = packed_ref.shape[0] // MINI
     row = lax.broadcasted_iota(jnp.int32, (MINI, LANES), 0)
     offsets = jnp.zeros((MINI, LANES), jnp.int32)
     for e in range(blocks):
@@ -120,18 +135,21 @@
                 ]
                 for odd in range(2)
             ]
-            for b in range(count + 1):
+            for b in range(count):
                 value = jnp.zeros((block_rows, LANES), jnp.float32)
-                low = count if b == count else b % (count // 2) * 2
+                low = b % (count // 2) * 2
                 for v in range(max(low, 1), min(low + 3, count) + 1):
-                    if b == count:
-                        source = jnp.where(tall_lane < LANES // 2, taken[0][v - 1], taken[1][v - 1])
-                    else:
-                        source = taken[b // (count // 2)][v - 1]
-                    value = jnp.where(index[b] == v, source, value)
-                at = b * height + c * blocks * share + e * share
+                    value = jnp.where(index[b] == v, taken[b // (count // 2)][v - 1], value)
+                at = b * tall + (c * blocks + e) * share
                 for q in range(MINI):
-                    packed_ref[slots[q], at : at + share, :] = value[q * share : (q + 1) * share]
+                    packed_ref[pl.ds(slots[q] * height + at, share), :] = value[q * share : (q + 1) * share]
+    rest = tails(
+        lambda c, e: tile_ref[c, e * block_rows : (e + 1) * block_rows, cols - LANES : cols],
+        lambda e: shift_ref[0, e] + SMAX,
+        count, tall_lane, cols, blocks, share,
+    )
+    for q in range(MINI):
+        packed_ref[pl.ds(slots[q] * height + count * tall, 1), :] = rest[q * share : q * share + 1]
 
 
 def rim_kernel(slot_ref, shift_ref, other_ref, packed_ref, out_ref):
@@ -139,19 +157,22 @@
     blocks = shift_ref.shape[0] - 1
     block_rows = rows // blocks
     share = block_rows // MINI
-    height = 2 * blocks * share
+    tall = 2 * blocks * share
+    height = packed_ref.shape[0] // MINI
     count = cols // LANES
     first = lax.axis_index("strip") == 0
     lane = lax.broadcasted_iota(jnp.int32, (MINI, LANES), 1)
     tall_lane = lax.broadcasted_iota(jnp.int32, (block_rows, LANES), 1)
-    moved = []
+    rim_of, shift_of, moved = {}, [], []
+    for e in range(blocks):
+        shift_of.append(jnp.concatenate([shift_ref[e]] * (block_rows // MINI), axis=0))
     for c in range(2):
         for e in range(blocks):
             lines = pl.ds(e * block_rows, block_rows)
             rim = jnp.where(first, other_ref[c, lines, 0:LANES], other_ref[c, lines, cols - LANES : cols])
-            shift = jnp.concatenate([shift_ref[e]] * (block_rows // MINI), axis=0)
-            lanes, _ = sources(shift, tall_lane, cols)
+            lanes, _ = sources(shift_of[e], tall_lane, cols)
             moved.append([jnp.take_along_axis(rim, lanes[odd], axis=1) for odd in range(2)])
+            rim_of[c, e] = rim
     pieces = [
         [jnp.concatenate([m[odd][q * share : (q + 1) * share] for m in moved], axis=0) for q in range(MINI)]
         for odd in range(2)
@@ -159,16 +180,23 @@
     _, index = sources(shift_ref[blocks], lane, cols)
     wanted = jnp.where(first, count + 1, 0)
     masks = [piece == wanted for piece in index]
+    rest = tails(
+        lambda c, e: rim_of[c, e], lambda e: shift_of[e], wanted, tall_lane, cols, blocks, share
+    )
+    slot = lax.broadcasted_iota(jnp.int32, (MINI, LANES), 0)
+    ends = jnp.zeros((MINI, LANES), jnp.float32)
+    for q in range(MINI):
+        ends = jnp.where(slot == slot_ref[q], rest[q * share : q * share + 1], ends)
     for j in range(MINI):
         rims = [pieces[odd][0] for odd in range(2)]
         for q in range(1, MINI):
             hit = slot_ref[q] == j
             rims = [jnp.where(hit, pieces[odd][q], rims[odd]) for odd in range(2)]
-        rims.append(jnp.where(lane < LANES // 2, rims[0], rims[1]))
         for b, mask in enumerate(masks):
-            at = slice(b * height, (b + 1) * height)
-            rim = rims[2 if b == count else b // (count // 2)]
-            out_ref[j, at, :] = jnp.where(mask, rim, packed_ref[j, at, :])
+            at = slice(j * height + b * tall, j * height + (b + 1) * tall)
+            out_ref[at, :] = jnp.where(mask, rims[b // (count // 2)], packed_ref[at, :])
+        at = slice((j + 1) * height - 1, (j + 1) * height)
+        out_ref[at, :] = packed_ref[at, :] + ends[j : j + 1]
 
 
 def partner(value, stride):
@@ -183,8 +211,8 @@
 def link_kernel(tap_ref, coef_ref, data_ref, out_ref):
     blocks = 2
     nb = 2 * out_ref.shape[2] // blocks // LANES
-    height = 4 * blocks
-    stride = (nb + 1) * height
+    tall = 4 * blocks
+    stride = nb * tall + 1
     lane = lax.broadcasted_iota(jnp.int32, (MINI, LANES), 1)
     date = lax.broadcasted_iota(jnp.int32, (MINI, LANES), 0)
     place_of = jnp.zeros((MINI, LANES), jnp.int32)
@@ -198,18 +226,18 @@
 
     def sums_of(e, h):
         sums = None
+        ends = load(nb * tall)
         for p in range(2):
             pieces = []
             for c in range(2):
                 row = (c * blocks + e) * 2 + p
-                tail = load(nb * height + row)
                 for odd in range(2):
                     block = odd * (nb // 2) + h
                     if h + 1 < nb // 2:
-                        there = load((block + 1) * height + row)
+                        there = load((block + 1) * tall + row)
                     else:
-                        there = pltpu.roll(tail, LANES // 2, 1) if odd else tail
-                    pieces.append((load(block * height + row), there))
+                        there = pltpu.roll(ends, (LANES - (2 * row + odd) * REACH) % LANES, 1)
+                    pieces.append((load(block * tall + row), there))
             cache = {}
 
             def at(c, l):
@@ -307,7 +335,7 @@
         slots = jnp.arange(MINI, dtype=jnp.int32)
         freq = lax.dynamic_slice_in_dim(center_freq, position // MINI * MINI, MINI)
     tall = 2 * blocks * share
-    height = tall * (cols // LANES + 1)
+    height = tall * (cols // LANES) + 1
     tile = (MINI, LANES)
     coefs, taps, slot_marks, shift_marks, packed = pl.pallas_call(
         prep_kernel,
@@ -316,7 +344,7 @@
             jax.ShapeDtypeStruct((REACH + 1,) + tile, jnp.float32),
             jax.ShapeDtypeStruct((MINI,) + tile, jnp.int32),
             jax.ShapeDtypeStruct((blocks + 1,) + tile, jnp.int32),
-            jax.ShapeDtypeStruct((MINI, height, LANES), jnp.float32),
+            jax.ShapeDtypeStruct((MINI * height, LANES), jnp.float32),
         ),
         in_specs=[hbm()] * 5,
         out_specs=(vmem(),) * 5,
@@ -342,7 +370,7 @@
     )(slot_marks, shift_marks, other_tile, packed)
     stacks = [[g + member for member in ORDER] for g in range(0, date_count, MINI)]
     data = lax.all_to_all(
-        packed, "date", split_axis=0, concat_axis=0, axis_index_groups=stacks, tiled=True
+        packed.reshape(MINI, 1, height * LANES), "date", split_axis=0, concat_axis=0, axis_index_groups=stacks, tiled=True
     )
     linked = pl.pallas_call(
         link_kernel,

time: 14.9 us -> 14.6 us (0.980)
  blocking collectives: 11.4 us -> 11.1 us
    all_to_all x1, blocking collectives: 11.4 us -> 11.1 us  [shards(): lax.all_to_all(packed.reshape(MINI, 1, height * LANES), 'date', split_axi...]
where the time goes in v6:
time: 14.6 us; the launch traced here: 14.5 us
  blocking collectives  11.1 us (76%)
  Pallas kernels  2.81 us (19%)
  starting transfers between devices  0.49 us (3%)
    all_to_all x1, blocking collectives, shards(): lax.all_to_all(packed.reshape(MINI, 1, height * LANES), 'date', split_axi...  11.1 us
    pallas_call x1, Pallas kernels, shards(): pl.pallas_call(link_kernel, out_shape=jax.ShapeDtypeStruct((2, MINI, bloc...  1.51 us
    pallas_call x1, Pallas kernels, shards(): pl.pallas_call(prep_kernel, out_shape=(jax.ShapeDtypeStruct((2 * ROUNDS *...  1.14 us
    ppermute x1, starting transfers between devices, shards(): lax.ppermute(own_tile, 'strip', [(s, strips - 1 - s) for s in range(strip...  0.49 us
  transfers between devices with their start and end apart: 1, of which 1 were waited for; matrix products, arithmetic and copies ran while one was open for 0% of the time, Pallas kernels for 8%

profile of v6, /device:TPU:0, one launch (start us, length us, event | category | flops | bytes accessed | tf_op | source)
XLA Modules:
  0.0 14.5 jit_solution(12353517361675627162)
XLA Ops:
  0.0 0.5 %collective-permute-start = (f32[2,32,512]{2,1,0:T(8,128)}, f32[2,32,512]{2,1,0:T(8,128)S(1)}, u32[]{:S(2)}, u32[]{:S(2)}) collective-permute-start(f32[2,32,512]{2,1,0:T(8,128)} %bitcast.5), channel_id=1, source_target_pairs={{0,1},{1,0},{2,3},{3,2},{4,5},{5,4},{6,7},{7,6},{8,9},{9,8},{10,11... | collective-permute-start | bytes 393224 | tf_op jit(solution)/shard_map/ppermute | solution.py:331
  0.5 1.1 %prep.1 = (f32[48,8,128]{2,1,0:T(8,128)S(1)}, f32[9,8,128]{2,1,0:T(8,128)S(1)}, s32[8,8,128]{2,1,0:T(8,128)S(1)}, s32[3,8,128]{2,1,0:T(8,128)S(1)}, f32[264,128]{1,0:T(8,128)S(1)}) custom-call(f32[8]{0:T(128)} %freq_hbm.1, f32[17]{0:T(128)} %tap_hbm.1, s32[8]{0:T(128)} %slot_hbm.1, s32[1,2]{1,0:T(1,128)} %shift_hbm.1, f32[2,32,512]{2,1,0:T(8,128)} %bitcast.6), custom_call_target="tpu_custom_call" | custom-call | tf_op jit(solution)/shard_map/prep/pallas_call | solution.py:340
  1.6 0.1 collective-permute-done.other_ref
  1.7 0.2 %rim.1 = f32[264,128]{1,0:T(8,128)S(1)} custom-call(s32[8,8,128]{2,1,0:T(8,128)S(1)} %get-tuple-element.12.slot_ref, s32[3,8,128]{2,1,0:T(8,128)S(1)} %get-tuple-element.13.shift_ref, f32[2,32,512]{2,1,0:T(8,128)S(1)} %collective-permute-done.other_ref, f32[264,128]{1,0:T(8,128)S(1)} %get-tuple-element.14.packed_ref), custom_call_target="tpu_custom_call", output_to_operand_aliasing={{}: (3, {})} | custom-call | tf_op jit(solution)/shard_map/rim/pallas_call | solution.py:362
  1.9 11.1 %all_to_all.5 = f32[8,1,4224]{2,1,0:T(1,128)S(1)} all-to-all(f32[8,1,4224]{2,1,0:T(1,128)S(1)} %bitcast.3), channel_id=1, replica_groups={{10,14,6,8,0,12,2,4},{11,15,7,9,1,13,3,5},{26,30,22,24,16,28,18,20},{27..., dimensions={0} | all-to-all | bytes 270336 | tf_op jit(solution)/shard_map/all_to_all | solution.py:372
  12.9 1.5 %link.1 = f32[2,8,512]{2,1,0:T(8,128)} custom-call(f32[9,8,128]{2,1,0:T(8,128)S(1)} %get-tuple-element.10.tap_ref, f32[48,8,128]{2,1,0:T(8,128)S(1)} %get-tuple-element.11.coef_ref, f32[264,128]{1,0:T(8,128)S(1)} %bitcast.4), custom_call_target="tpu_custom_call" | custom-call | tf_op jit(solution)/shard_map/link/pallas_call | solution.py:375
Async XLA Ops:
  0.0 1.7 %collective-permute-start = (f32[2,32,512]{2,1,0:T(8,128)}, f32[2,32,512]{2,1,0:T(8,128)S(1)}, u32[]{:S(2)}, u32[]{:S(2)}) collective-permute-start(f32[2,32,512]{2,1,0:T(8,128)} %bitcast.5), channel_id=1, source_target_pairs={{0,1},{1,0},{2,3},{3,2},{4,5},{5,4},{6,7},{7,6},{8,9},{9,8},{10,11... | collective-permute-start | bytes 393224 | tf_op jit(solution)/shard_map/ppermute | solution.py:331

commit v7 on v6

--- a/solution.py
+++ b/solution.py
@@ -31,6 +31,14 @@
 
 def params():
     return pltpu.CompilerParams(vmem_limit_bytes=VMEM_LIMIT)
+
+
+def table(entries, shape):
+    row = lax.broadcasted_iota(jnp.int32, shape, 0)
+    result = jnp.full(shape, entries[0], jnp.int32)
+    for i, entry in enumerate(entries[1:], 1):
+        result = jnp.where(row == i, entry, result)
+    return result
 
 
 def sources(shift, lane, cols):
@@ -74,7 +82,7 @@
     ]
     for copy in copies:
         copy.start()
-    date = lax.broadcasted_iota(jnp.int32, (MINI, LANES), 0)
+    date = table(ORDER, (MINI, LANES))
     lane = lax.broadcasted_iota(jnp.int32, (MINI, LANES), 1)
     for copy in copies[:4]:
         copy.wait()
@@ -100,10 +108,10 @@
     cosine, sine = jnp.cos(angle), jnp.sin(angle)
     taps = [jnp.full((MINI, LANES), tap_ref[t], jnp.float32) for t in range(TAPS)]
     for j in range(ROUNDS * REACH):
-        tap = taps[REACH + 1 + j % REACH]
+        tap = 0.5 * taps[REACH + 1 + j % REACH]
         coef_ref[2 * j] = tap * jnp.broadcast_to(cosine[:, j : j + 1], (MINI, LANES))
         coef_ref[2 * j + 1] = tap * jnp.broadcast_to(sine[:, j : j + 1], (MINI, LANES))
-    tap_out[0] = taps[REACH]
+    tap_out[0] = 0.5 * taps[REACH]
     for k in range(1, REACH + 1):
         tap_out[k] = taps[REACH - k] / taps[REACH + k]
     for q in range(MINI):
@@ -200,12 +208,8 @@
 
 
 def partner(value, stride):
-    if 2 * stride == MINI:
-        return pltpu.roll(value, stride, 0)
-    date = lax.broadcasted_iota(jnp.int32, value.shape, 0)
-    up = pltpu.roll(value, MINI - stride, 0)
-    down = pltpu.roll(value, stride, 0)
-    return jnp.where((date // stride) % 2 == 0, up, down)
+    places = [ORDER.index(member ^ stride) for member in ORDER]
+    return jnp.take_along_axis(value, table(places, value.shape), axis=0)
 
 
 def link_kernel(tap_ref, coef_ref, data_ref, out_ref):
@@ -214,15 +218,10 @@
     tall = 4 * blocks
     stride = nb * tall + 1
     lane = lax.broadcasted_iota(jnp.int32, (MINI, LANES), 1)
-    date = lax.broadcasted_iota(jnp.int32, (MINI, LANES), 0)
-    place_of = jnp.zeros((MINI, LANES), jnp.int32)
-    for place, member in enumerate(ORDER):
-        place_of = jnp.where(date == member, place, place_of)
-    even_lane = 2 * lane % LANES
+    by_date = table([ORDER.index(d) for d in range(MINI)], (MINI, LANES))
 
     def load(row):
-        arrived = data_ref[pl.ds(row, MINI, stride=stride), :]
-        return jnp.take_along_axis(arrived, place_of, axis=0)
+        return data_ref[pl.ds(row, MINI, stride=stride), :]
 
     def sums_of(e, h):
         sums = None
@@ -283,7 +282,8 @@
         return 1.0 / jnp.maximum(length, 1.0)
 
     for g in range(blocks * nb // 2):
-        field = [total * 0.25 for total in sums_of(g // (nb // 2), g % (nb // 2))]
+        field = sums_of(g // (nb // 2), g % (nb // 2))
+        field[-1] = field[-1] * 0.25
         vec_re = field[-1] + (field[0] + field[2] + field[4])
         vec_im = field[1] + field[3] + field[5]
         energies = [energy_of(vec_re, vec_im)]
@@ -300,8 +300,8 @@
         factor = 1.0
         for energy in energies:
             factor = factor * shrink(jnp.sqrt(energy) * factor)
-        out_ref[0, :, pl.ds(g * LANES, LANES)] = vec_re * factor
-        out_ref[1, :, pl.ds(g * LANES, LANES)] = vec_im * factor
+        for c, vec in enumerate((vec_re, vec_im)):
+            out_ref[c, :, pl.ds(g * LANES, LANES)] = jnp.take_along_axis(vec * factor, by_date, axis=0)
 
 
 def to_owners(linked, inverse, blocks):

time: 14.6 us -> 14.6 us (level)
  transfers between devices with their start and end apart: 1 -> 1, of which waited for: 1 -> 0; matrix products, arithmetic and copies ran while one was open for 0% -> 0% of each run, Pallas kernels for 8% -> 8%
where the time goes in v7:
time: 14.6 us; the launch traced here: 14.4 us
  blocking collectives  11.1 us (76%)
  Pallas kernels  2.79 us (19%)
  starting transfers between devices  0.49 us (3%)
    all_to_all x1, blocking collectives, shards(): lax.all_to_all(packed.reshape(MINI, 1, height * LANES), 'date', split_axi...  11.1 us
    pallas_call x1, Pallas kernels, shards(): pl.pallas_call(link_kernel, out_shape=jax.ShapeDtypeStruct((2, MINI, bloc...  1.49 us
    pallas_call x1, Pallas kernels, shards(): pl.pallas_call(prep_kernel, out_shape=(jax.ShapeDtypeStruct((2 * ROUNDS *...  1.14 us
    ppermute x1, starting transfers between devices, shards(): lax.ppermute(own_tile, 'strip', [(s, strips - 1 - s) for s in range(strip...  0.49 us
  transfers between devices with their start and end apart: 1, of which 0 were waited for; matrix products, arithmetic and copies ran while one was open for 0% of the time, Pallas kernels for 8%

profile of v7, /device:TPU:0, one launch (start us, length us, event | category | flops | bytes accessed | tf_op | source)
XLA Modules:
  0.0 14.4 jit_solution(8564540748447195458)
XLA Ops:
  0.0 0.5 %collective-permute-start = (f32[2,32,512]{2,1,0:T(8,128)}, f32[2,32,512]{2,1,0:T(8,128)S(1)}, u32[]{:S(2)}, u32[]{:S(2)}) collective-permute-start(f32[2,32,512]{2,1,0:T(8,128)} %bitcast.5), channel_id=1, source_target_pairs={{0,1},{1,0},{2,3},{3,2},{4,5},{5,4},{6,7},{7,6},{8,9},{9,8},{10,11... | collective-permute-start | bytes 393224 | tf_op jit(solution)/shard_map/ppermute | solution.py:331
  0.5 1.1 %prep.1 = (f32[48,8,128]{2,1,0:T(8,128)S(1)}, f32[9,8,128]{2,1,0:T(8,128)S(1)}, s32[8,8,128]{2,1,0:T(8,128)S(1)}, s32[3,8,128]{2,1,0:T(8,128)S(1)}, f32[264,128]{1,0:T(8,128)S(1)}) custom-call(f32[8]{0:T(128)} %freq_hbm.1, f32[17]{0:T(128)} %tap_hbm.1, s32[8]{0:T(128)} %slot_hbm.1, s32[1,2]{1,0:T(1,128)} %shift_hbm.1, f32[2,32,512]{2,1,0:T(8,128)} %bitcast.6), custom_call_target="tpu_custom_call" | custom-call | tf_op jit(solution)/shard_map/prep/pallas_call | solution.py:340
  1.6 0.1 collective-permute-done.other_ref
  1.7 0.2 %rim.1 = f32[264,128]{1,0:T(8,128)S(1)} custom-call(s32[8,8,128]{2,1,0:T(8,128)S(1)} %get-tuple-element.12.slot_ref, s32[3,8,128]{2,1,0:T(8,128)S(1)} %get-tuple-element.13.shift_ref, f32[2,32,512]{2,1,0:T(8,128)S(1)} %collective-permute-done.other_ref, f32[264,128]{1,0:T(8,128)S(1)} %get-tuple-element.14.packed_ref), custom_call_target="tpu_custom_call", output_to_operand_aliasing={{}: (3, {})} | custom-call | tf_op jit(solution)/shard_map/rim/pallas_call | solution.py:362
  1.9 11.1 %all_to_all.5 = f32[8,1,4224]{2,1,0:T(1,128)S(1)} all-to-all(f32[8,1,4224]{2,1,0:T(1,128)S(1)} %bitcast.3), channel_id=1, replica_groups={{10,14,6,8,0,12,2,4},{11,15,7,9,1,13,3,5},{26,30,22,24,16,28,18,20},{27..., dimensions={0} | all-to-all | bytes 270336 | tf_op jit(solution)/shard_map/all_to_all | solution.py:372
  12.9 1.5 %link.1 = f32[2,8,512]{2,1,0:T(8,128)} custom-call(f32[9,8,128]{2,1,0:T(8,128)S(1)} %get-tuple-element.10.tap_ref, f32[48,8,128]{2,1,0:T(8,128)S(1)} %get-tuple-element.11.coef_ref, f32[264,128]{1,0:T(8,128)S(1)} %bitcast.4), custom_call_target="tpu_custom_call" | custom-call | tf_op jit(solution)/shard_map/link/pallas_call | solution.py:375
Async XLA Ops:
  0.0 1.7 %collective-permute-start = (f32[2,32,512]{2,1,0:T(8,128)}, f32[2,32,512]{2,1,0:T(8,128)S(1)}, u32[]{:S(2)}, u32[]{:S(2)}) collective-permute-start(f32[2,32,512]{2,1,0:T(8,128)} %bitcast.5), channel_id=1, source_target_pairs={{0,1},{1,0},{2,3},{3,2},{4,5},{5,4},{6,7},{7,6},{8,9},{9,8},{10,11... | collective-permute-start | bytes 393224 | tf_op jit(solution)/shard_map/ppermute | solution.py:331

commit v8 on v7

--- a/solution.py
+++ b/solution.py
@@ -12,7 +12,7 @@
 ITERS = 3
 LANES = 128
 REACH = TAPS // 2
-ORDER = (5, 7, 3, 4, 0, 6, 1, 2)
+ORDER = (5, 6, 3, 2, 0, 7, 4, 1)
 LANE_BITS = LANES.bit_length() - 1
 VMEM_LIMIT = 16 * 1024 * 1024
 
@@ -187,7 +187,8 @@
     ]
     _, index = sources(shift_ref[blocks], lane, cols)
     wanted = jnp.where(first, count + 1, 0)
-    masks = [piece == wanted for piece in index]
+    block = jnp.where(first, count // 2 - 1, 0)
+    masks = [index[odd * (count // 2)] + 2 * block == wanted for odd in range(2)]
     rest = tails(
         lambda c, e: rim_of[c, e], lambda e: shift_of[e], wanted, tall_lane, cols, blocks, share
     )
@@ -200,9 +201,9 @@
         for q in range(1, MINI):
             hit = slot_ref[q] == j
             rims = [jnp.where(hit, pieces[odd][q], rims[odd]) for odd in range(2)]
-        for b, mask in enumerate(masks):
-            at = slice(j * height + b * tall, j * height + (b + 1) * tall)
-            out_ref[at, :] = jnp.where(mask, rims[b // (count // 2)], packed_ref[at, :])
+        for odd in range(2):
+            at = pl.ds(j * height + (odd * (count // 2) + block) * tall, tall)
+            out_ref[at, :] = jnp.where(masks[odd], rims[odd], packed_ref[at, :])
         at = slice((j + 1) * height - 1, (j + 1) * height)
         out_ref[at, :] = packed_ref[at, :] + ends[j : j + 1]
 

time: 14.6 us -> 14.6 us (level)
  no operation moved by 1% of the time
where the time goes in v8:
time: 14.6 us; the launch traced here: 14.4 us
  blocking collectives  11.1 us (76%)
  Pallas kernels  2.78 us (19%)
  starting transfers between devices  0.49 us (3%)
    all_to_all x1, blocking collectives, shards(): lax.all_to_all(packed.reshape(MINI, 1, height * LANES), 'date', split_axi...  11.1 us
    pallas_call x1, Pallas kernels, shards(): pl.pallas_call(link_kernel, out_shape=jax.ShapeDtypeStruct((2, MINI, bloc...  1.49 us
    pallas_call x1, Pallas kernels, shards(): pl.pallas_call(prep_kernel, out_shape=(jax.ShapeDtypeStruct((2 * ROUNDS *...  1.14 us
    ppermute x1, starting transfers between devices, shards(): lax.ppermute(own_tile, 'strip', [(s, strips - 1 - s) for s in range(strip...  0.49 us
  transfers between devices with their start and end apart: 1, of which 0 were waited for; matrix products, arithmetic and copies ran while one was open for 0% of the time, Pallas kernels for 8%

profile of v8, /device:TPU:0, one launch (start us, length us, event | category | flops | bytes accessed | tf_op | source)
XLA Modules:
  0.0 14.4 jit_solution(3673798146484559856)
XLA Ops:
  0.0 0.5 %collective-permute-start = (f32[2,32,512]{2,1,0:T(8,128)}, f32[2,32,512]{2,1,0:T(8,128)S(1)}, u32[]{:S(2)}, u32[]{:S(2)}) collective-permute-start(f32[2,32,512]{2,1,0:T(8,128)} %bitcast.5), channel_id=1, source_target_pairs={{0,1},{1,0},{2,3},{3,2},{4,5},{5,4},{6,7},{7,6},{8,9},{9,8},{10,11... | collective-permute-start | bytes 393224 | tf_op jit(solution)/shard_map/ppermute | solution.py:332
  0.5 1.1 %prep.1 = (f32[48,8,128]{2,1,0:T(8,128)S(1)}, f32[9,8,128]{2,1,0:T(8,128)S(1)}, s32[8,8,128]{2,1,0:T(8,128)S(1)}, s32[3,8,128]{2,1,0:T(8,128)S(1)}, f32[264,128]{1,0:T(8,128)S(1)}) custom-call(f32[8]{0:T(128)} %freq_hbm.1, f32[17]{0:T(128)} %tap_hbm.1, s32[8]{0:T(128)} %slot_hbm.1, s32[1,2]{1,0:T(1,128)} %shift_hbm.1, f32[2,32,512]{2,1,0:T(8,128)} %bitcast.6), custom_call_target="tpu_custom_call" | custom-call | tf_op jit(solution)/shard_map/prep/pallas_call | solution.py:341
  1.6 0.1 collective-permute-done.other_ref
  1.7 0.2 %rim.1 = f32[264,128]{1,0:T(8,128)S(1)} custom-call(s32[8,8,128]{2,1,0:T(8,128)S(1)} %get-tuple-element.12.slot_ref, s32[3,8,128]{2,1,0:T(8,128)S(1)} %get-tuple-element.13.shift_ref, f32[2,32,512]{2,1,0:T(8,128)S(1)} %collective-permute-done.other_ref, f32[264,128]{1,0:T(8,128)S(1)} %get-tuple-element.14.packed_ref), custom_call_target="tpu_custom_call", output_to_operand_aliasing={{}: (3, {})} | custom-call | tf_op jit(solution)/shard_map/rim/pallas_call | solution.py:363
  1.9 11.1 %all_to_all.5 = f32[8,1,4224]{2,1,0:T(1,128)S(1)} all-to-all(f32[8,1,4224]{2,1,0:T(1,128)S(1)} %bitcast.3), channel_id=1, replica_groups={{10,12,6,4,0,14,8,2},{11,13,7,5,1,15,9,3},{26,28,22,20,16,30,24,18},{27..., dimensions={0} | all-to-all | bytes 270336 | tf_op jit(solution)/shard_map/all_to_all | solution.py:373
  12.9 1.5 %link.1 = f32[2,8,512]{2,1,0:T(8,128)} custom-call(f32[9,8,128]{2,1,0:T(8,128)S(1)} %get-tuple-element.10.tap_ref, f32[48,8,128]{2,1,0:T(8,128)S(1)} %get-tuple-element.11.coef_ref, f32[264,128]{1,0:T(8,128)S(1)} %bitcast.4), custom_call_target="tpu_custom_call" | custom-call | tf_op jit(solution)/shard_map/link/pallas_call | solution.py:376
Async XLA Ops:
  0.0 1.7 %collective-permute-start = (f32[2,32,512]{2,1,0:T(8,128)}, f32[2,32,512]{2,1,0:T(8,128)S(1)}, u32[]{:S(2)}, u32[]{:S(2)}) collective-permute-start(f32[2,32,512]{2,1,0:T(8,128)} %bitcast.5), channel_id=1, source_target_pairs={{0,1},{1,0},{2,3},{3,2},{4,5},{5,4},{6,7},{7,6},{8,9},{9,8},{10,11... | collective-permute-start | bytes 393224 | tf_op jit(solution)/shard_map/ppermute | solution.py:332
